TPU v7x, 128 devices: a whole 4x4x4 slice. The times are simulated.
128 devices in a mesh: row: 16 (over y, x), col: 8 (over z, core).
Axes of the slice: x: 4, y: 4, z: 4, core: 2. Of those that a mesh axis runs over, the one named last changes fastest.
Arguments:
- row_emb: float32 [128, 300, 1024], P(('row', 'col')), may hold values from -1.5 to 1.5
- col_emb: float32 [128, 300, 1024], P(('row', 'col')), may hold values from -1.5 to 1.5
- row_acc: float32 [128, 300, 1024], P(('row', 'col')), may hold values from 0.5 to 8
- col_acc: float32 [128, 300, 1024], P(('row', 'col')), may hold values from 0.5 to 8
- marginal_log: float32 [131072], replicated, may hold values from -2 to 1
- tile_rows: int32 [384], P(('row', 'col')), may hold values from 0 to 127, as said below
- tile_cols: int32 [384], P(('row', 'col')), may hold values from 0 to 127, as said below
- counts: int32 [384, 1024, 1024], P(('row', 'col')), may hold values from 0 to 2047
Outputs:
- new_row_emb: float32 [128, 300, 1024], P(('row', 'col'))
- new_col_emb: float32 [128, 300, 1024], P(('row', 'col'))
- new_row_acc: float32 [128, 300, 1024], P(('row', 'col'))
- new_col_acc: float32 [128, 300, 1024], P(('row', 'col'))
Inputs may be any that keep to these rules, and one draw needn't show every extreme that they name: Block g of the embeddings lies on device g in the mesh's order (row slowest). Slot k lies on device p = k // 3; with p at row index r and col index c, tile_rows[k] // 8 equals r. With slot k on the device at col index c, tile_cols[k] % 8 equals c.
All inputs are finite; a program needn't handle non-finite values.
Results may differ from a plain program's by a relative error of at most 0.019.
Values may be sent and summed in bfloat16 or wider, within the bound.
No kernel may reach another device: no remote copies, remote signals or barrier semaphores. Data moves between devices by JAX's collectives and lax.ppermute only.
A program may use at most 128 MiB of HBM per device.

v0:
```python
import jax
import jax.numpy as jnp
from jax import lax
from jax.sharding import PartitionSpec as P

err_scale = 0.03125
learn_rate = 0.1


def split_up(array, dim, length):
    before, after = (array.shape[:dim], array.shape[dim + 1 :])
    return jnp.moveaxis(array.reshape(*before, length, -1, *after), dim, 0)


def sum_at_owner(array, axis, dim):
    length = lax.axis_size(axis)
    pieces = lax.all_to_all(split_up(array, dim, length), axis, 0, 0, tiled=True)
    return jnp.sum(pieces.astype(jnp.float32), axis=0)


def tile_terms(row_block, col_block, tile_counts, row_margin, col_margin):
    scores = lax.dot_general(
        row_block, col_block, (((0,), (0,)), ((), ())), preferred_element_type=jnp.float32
    )
    counted = tile_counts.astype(jnp.float32)
    shifted_log = jnp.log(jnp.maximum(counted, 1.0)) - row_margin[:, None] - col_margin[None, :]
    residue = scores - shifted_log
    weighted = (0.1 + 0.25 * jnp.sqrt(counted)) * residue
    cell_grad = jnp.where(tile_counts > 0, weighted, jax.nn.sigmoid(residue)) * err_scale
    errors = cell_grad.astype(jnp.bfloat16)
    row_term = lax.dot_general(
        col_block, errors, (((1,), (1,)), ((), ())), preferred_element_type=jnp.float32
    )
    col_term = jnp.dot(row_block, errors, preferred_element_type=jnp.float32)
    return (row_term, col_term)


def add_slot(buffer, slot_index, term):
    old_value = lax.dynamic_index_in_dim(buffer, slot_index, 0, keepdims=False)
    return lax.dynamic_update_index_in_dim(buffer, old_value + term, slot_index, 0)


def adagrad(weights, history, gradient):
    grown = history + gradient * gradient
    return (weights - learn_rate * gradient / jnp.sqrt(grown), grown)


def body(row_emb, col_emb, row_acc, col_acc, marginal_log, tile_rows, tile_cols, counts):
    col_count = lax.axis_size("col")
    row_count = lax.axis_size("row")
    emb_width = row_emb.shape[1]
    block_len = row_emb.shape[2]
    tile_total = counts.shape[0]
    row_low = row_emb.astype(jnp.bfloat16)
    col_low = col_emb.astype(jnp.bfloat16)
    rows_near = lax.all_gather(row_low, "col", axis=0, tiled=True)
    grads = (
        jnp.zeros((col_count, emb_width, block_len), jnp.float32),
        jnp.zeros((row_count, emb_width, block_len), jnp.float32),
    )
    cols_near = lax.all_gather(col_low, "row", axis=0, tiled=True)
    for tile_slot in range(tile_total):
        col_slot = tile_cols[tile_slot] // col_count
        col_block = lax.dynamic_index_in_dim(cols_near, col_slot, 0, keepdims=False)
        row_id = tile_rows[tile_slot]
        col_id = tile_cols[tile_slot]
        row_slot = row_id % col_count
        apply_col_slot = col_id // col_count
        row_block = lax.dynamic_index_in_dim(rows_near, row_slot, 0, keepdims=False)
        row_margin = lax.dynamic_slice_in_dim(marginal_log, row_id * block_len, block_len)
        col_margin = lax.dynamic_slice_in_dim(marginal_log, col_id * block_len, block_len)
        row_term, col_term = tile_terms(
            row_block, col_block, counts[tile_slot], row_margin, col_margin
        )
        grads = (
            add_slot(grads[0], row_slot, row_term),
            add_slot(grads[1], apply_col_slot, col_term),
        )
    row_sum = sum_at_owner(grads[0].astype(jnp.bfloat16), "col", 0)
    col_sum = lax.psum_scatter(
        grads[1].astype(jnp.bfloat16), "row", scatter_dimension=0, tiled=True
    ).astype(jnp.float32)
    new_row_emb, new_row_acc = adagrad(row_emb, row_acc, row_sum)
    new_col_emb, new_col_acc = adagrad(col_emb, col_acc, col_sum)
    return (new_row_emb, new_col_emb, new_row_acc, new_col_acc)


def solution(mesh):
    placed = (
        P(("row", "col"), None, None),
        P(("row", "col"), None, None),
        P(("row", "col"), None, None),
        P(("row", "col"), None, None),
        P(),
        P(("row", "col")),
        P(("row", "col")),
        P(("row", "col"), None, None),
    )
    return jax.shard_map(
        body,
        mesh=mesh,
        in_specs=placed,
        out_specs=(
            P(("row", "col"), None, None),
            P(("row", "col"), None, None),
            P(("row", "col"), None, None),
            P(("row", "col"), None, None),
        ),
        check_vma=False,
    )
```

profile of v0, /device:TPU:0, one launch (start us, length us, event | category | flops | bytes accessed | tf_op | source)
XLA Modules:
  0.0 274.4 jit_solution(9816080059861527763)
XLA Ops:
  7.2 2.3 copy.28
  9.6 2.3 copy.29
  12.0 0.6 fusion.64
  20.0 0.6 fusion.63
  30.0 0.8 fusion.62
  30.8 17.6 %all-gather.5.cloned.1.call-done = bf16[8,300,1024]{2,1,0:T(8,128)(2,1)} async-done(((bf16[1,300,1024]{2,1,0:T(8,128)(2,1)}), bf16[8,300,1024]{2,1,0:T(8,128)(2,1)}) %all-gather.5.cloned.1.call-update) | async-done | bytes 4915216 | tf_op jit(solution)/shard_map/all_gather | solution.py:56
  48.3 80.5 %all-gather.3.cloned.1.call-done = bf16[16,300,1024]{2,1,0:T(8,128)(2,1)} async-done(((bf16[1,300,1024]{2,1,0:T(8,128)(2,1)}), bf16[16,300,1024]{2,1,0:T(8,128)(2,1)}) %all-gather.3.cloned.1.call-update) | async-done | bytes 9830416 | tf_op jit(solution)/shard_map/all_gather | solution.py:61
  128.8 8.2 %fusion.14 = bf16[1024,1024]{1,0:T(8,128)(2,1)} fusion(s32[3,1024,1024]{2,1,0:T(8,128)} %param.15, f32[1024]{0:T(1024)S(1)} %get-tuple-element.17, f32[1024]{0:T(1024)S(1)} %get-tuple-element.18, bf16[8,300,1024]{2,1,0:T(8,128)(2,1)} %all-gather.5.cloned.1.call-done, s32[]{:T(128)S(6)} %select_n.95, ...), kind=kOutput, calls=%fused_computation.22 | convolution fusion | flops 644874240 | bytes 7544840 | tf_op jit(solution)/shard_map/dot_general | solution.py:22
  137.0 9.2 %broadcast_in_dim.36 = f32[16,300,1024]{2,1,0:T(8,128)} broadcast(f32[]{:T(128)} %constant.108.clone.1), dimensions={} | broadcast | bytes 19660804 | tf_op jit(solution)/shard_map/broadcast_in_dim | solution.py:59
  146.2 2.9 %fusion.23 = f32[16,300,1024]{2,1,0:T(8,128)} fusion(f32[16,300,1024]{2,1,0:T(8,128)} %broadcast_in_dim.36, s32[]{:T(128)S(6)} %select_n.93, bf16[1024,1024]{1,0:T(8,128)(2,1)S(1)} %copy-done.8, bf16[8,300,1024]{2,1,0:T(8,128)(2,1)} %all-gather.5.cloned.1.call-done, s32[]{:T(128)S(6)} %select_n.95), kind=kOutput, calls=%fused_computation.38 | convolution fusion | flops 629145600 | bytes 3964936 | tf_op jit(solution)/shard_map/dot_general | solution.py:34
  149.2 1.5 constant_dynamic-slice_fusion.3
  150.8 5.6 %fusion.9 = bf16[1024,1024]{1,0:T(8,128)(2,1)S(1)} fusion(s32[3,1024,1024]{2,1,0:T(8,128)S(1)} %bitcast.136, f32[1024]{0:T(1024)S(1)} %get-tuple-element.15, f32[1024]{0:T(1024)S(1)} %get-tuple-element.16, bf16[8,300,1024]{2,1,0:T(8,128)(2,1)} %all-gather.5.cloned.1.call-done, s32[]{:T(128)S(6)} %select_n.100, ...), kind=kOutput, calls=%fused_computation.15 | convolution fusion | flops 644874240 | bytes 7544840 | tf_op jit(solution)/shard_map/dot_general | solution.py:22
  156.4 0.5 slice-done.4
  156.9 1.9 fusion.18
  158.9 5.6 %fusion.4 = bf16[1024,1024]{1,0:T(8,128)(2,1)S(1)} fusion(s32[3,1024,1024]{2,1,0:T(8,128)S(1)} %bitcast.136, f32[1024]{0:T(1024)S(1)} %get-tuple-element.19, f32[1024]{0:T(1024)S(1)} %get-tuple-element.14, bf16[8,300,1024]{2,1,0:T(8,128)(2,1)} %all-gather.5.cloned.1.call-done, s32[]{:T(128)S(6)} %select_n.107, ...), kind=kOutput, calls=%fused_computation.8 | convolution fusion | flops 644874240 | bytes 7544840 | tf_op jit(solution)/shard_map/dot_general | solution.py:22
  164.6 1.3 copy-done.2
  165.9 1.9 fusion.16
  167.8 5.0 %convert_element_type.49 = bf16[16,300,1024]{2,1,0:T(8,128)(2,1)} convert(f32[16,300,1024]{2,1,0:T(8,128)S(1)} %fusion.16) | non-fusion elementwise | flops 4915200 | bytes 29491200 | tf_op jit(solution)/shard_map/convert_element_type | solution.py:81
  172.8 1.3 broadcast_in_dim.32
  174.3 1.9 fusion.24
  176.4 2.1 fusion.22
  178.6 1.9 fusion.20
  180.5 0.8 convert_bitcast_fusion
  181.3 62.4 %all_to_all.5 = bf16[8,1,300,1024]{3,2,1,0:T(8,128)(2,1)S(1)} all-to-all(bf16[8,1,300,1024]{3,2,1,0:T(8,128)(2,1)S(1)} %convert_bitcast_fusion), channel_id=1, replica_groups=mesh['row'=16,'col'=8] {'col'}, dimensions={0} | all-to-all | bytes 9830400 | tf_op jit(solution)/shard_map/all_to_all | solution.py:17
  243.7 1.1 convert_reduce_fusion
  244.9 0.4 multiply_bitcast_fusion
  245.3 0.4 copy-done.4
  245.7 5.8 %multiply_subtract_fusion = (f32[1,300,1024]{2,0,1:T(1,128)}, f32[1,300,1024]{2,0,1:T(1,128)}) fusion(f32[1,300,1024]{2,0,1:T(1,128)S(1)} %copy-done, f32[300,1024]{1,0:T(8,128)S(1)} %get-tuple-element.13, f32[1,300,1024]{2,0,1:T(1,128)S(1)} %copy-done.4, f32[1,300,1024]{2,1,0:T(8,128)S(1)} %get-tuple-element.12), kind=kLoop, calls=%fused_computation.47 | loop fusion | flops 921600 | bytes 7372800 | tf_op jit(solution)/shard_map/sub | solution.py:45
  251.5 10.0 %reduce-scatter.4.cloned.1.call-done = bf16[1,300,1024]{2,1,0:T(8,128)(2,1)} async-done(((bf16[16,300,1024]{2,1,0:T(8,128)(2,1)}), bf16[1,300,1024]{2,1,0:T(8,128)(2,1)}) %reduce-scatter.4.cloned.1.call-update) | async-done | bytes 614416
  261.5 1.8 fusion.26
  263.3 2.3 copy.21
  265.6 2.3 copy.22
  (44 shorter events, 0.9 us)
Async XLA Ops:
  7.2 4.8 %copy-start.6 = (s32[3]{0:T(128)S(1)}, s32[3]{0:T(128)}, u32[]{:S(2)}) copy-start(s32[3]{0:T(128)} %param.13) | copy-start | bytes 40
  7.2 12.9 %copy-start.7 = (s32[3]{0:T(128)S(1)}, s32[3]{0:T(128)}, u32[]{:S(2)}) copy-start(s32[3]{0:T(128)} %param.14) | copy-start | bytes 40
  7.2 41.2 %all-gather.5.cloned.1.call-start = ((), (), s32[]{:S(2)}) async-start(), calls=%async_computation.3 | async-start | bytes 5603328 | tf_op jit(solution)/shard_map/all_gather | solution.py:56
  9.6 119.3 %all-gather.3.cloned.1.call-start = ((), (), s32[]{:S(2)}) async-start(), calls=%async_computation.2 | async-start | bytes 10584064 | tf_op jit(solution)/shard_map/all_gather | solution.py:61
  11.9 249.6 %reduce-scatter.4.cloned.1.call-start = ((), (), s32[]{:S(2)}) async-start(), calls=%async_computation.4 | async-start | bytes 10584064
  128.8 21.9 %slice-start.5 = ((s8[12582912]{0:T(1024)(128)(4,1)}), s8[4194304]{0:T(1024)(128)(4,1)S(1)}, s32[]{:S(2)}) async-start(s8[12582912]{0:T(1024)(128)(4,1)} %bitcast.135), calls=%async_computation.10 | async-start | bytes 8388608
  128.8 21.9 %slice-start.6 = ((s8[12582912]{0:T(1024)(128)(4,1)}), s8[4194304]{0:T(1024)(128)(4,1)S(1)}, s32[]{:S(2)}) async-start(s8[12582912]{0:T(1024)(128)(4,1)} %bitcast.135), calls=%async_computation.11 | async-start | bytes 8388608
  137.0 9.3 %copy-start.8 = (bf16[1024,1024]{1,0:T(8,128)(2,1)S(1)}, bf16[1024,1024]{1,0:T(8,128)(2,1)}, u32[]{:S(2)}) copy-start(bf16[1024,1024]{1,0:T(8,128)(2,1)} %fusion.14) | copy-start | bytes 6291460
  137.0 13.7 %slice-start.7 = ((s8[12582912]{0:T(1024)(128)(4,1)}), s8[4194304]{0:T(1024)(128)(4,1)S(1)}, s32[]{:S(2)}) async-start(s8[12582912]{0:T(1024)(128)(4,1)} %bitcast.135), calls=%async_computation.12 | async-start | bytes 8388608
  149.2 7.2 %slice-start = ((s8[19922944]{0:T(1024)(128)(4,1)}), s8[4194304]{0:T(1024)(128)(4,1)S(1)}, s32[]{:S(2)}) async-start(s8[19922944]{0:T(1024)(128)(4,1)} %bitcast.133), calls=%async_computation.5 | async-start | bytes 8388608
  150.7 5.6 %slice-start.1 = ((s8[19922944]{0:T(1024)(128)(4,1)}), s8[4194304]{0:T(1024)(128)(4,1)S(1)}, s32[]{:S(2)}) async-start(s8[19922944]{0:T(1024)(128)(4,1)} %bitcast.133), calls=%async_computation.6 | async-start | bytes 8388608
  150.8 5.6 %slice-start.2 = ((s8[19922944]{0:T(1024)(128)(4,1)}), s8[4194304]{0:T(1024)(128)(4,1)S(1)}, s32[]{:S(2)}) async-start(s8[19922944]{0:T(1024)(128)(4,1)} %bitcast.133), calls=%async_computation.7 | async-start | bytes 8388608
  150.8 5.6 %slice-start.3 = ((s8[19922944]{0:T(1024)(128)(4,1)}), s8[4194304]{0:T(1024)(128)(4,1)S(1)}, s32[]{:S(2)}) async-start(s8[19922944]{0:T(1024)(128)(4,1)} %bitcast.133), calls=%async_computation.8 | async-start | bytes 8388608
  150.8 6.1 %slice-start.4 = ((s8[19922944]{0:T(1024)(128)(4,1)}), s8[3145728]{0:T(1024)(128)(4,1)S(1)}, s32[]{:S(2)}) async-start(s8[19922944]{0:T(1024)(128)(4,1)} %bitcast.133), calls=%async_computation.9 | async-start | bytes 6291456
  164.5 1.3 copy-start.2
  172.8 1.6 copy-start.9
  176.4 2.2 copy-start.3
  243.7 1.5 copy-start
  243.7 2.0 copy-start.4
  245.2 16.3 %copy-start.1 = (f32[1,300,1024]{2,0,1:T(1,128)S(1)}, f32[1,300,1024]{2,0,1:T(1,128)}, u32[]{:S(2)}) copy-start(f32[1,300,1024]{2,0,1:T(1,128)} %param.9) | copy-start | bytes 3686404
  245.2 16.3 %copy-start.5 = (f32[1,300,1024]{2,0,1:T(1,128)S(1)}, f32[1,300,1024]{2,0,1:T(1,128)}, u32[]{:S(2)}) copy-start(f32[1,300,1024]{2,0,1:T(1,128)} %param.11) | copy-start | bytes 3686404
Sparse Core Ops, SparseCore 0:
  10.3 38.0 all-gather.4
  51.0 77.7 all-gather.2
  172.9 88.6 reduce-scatter.3
where the time goes:
time: 275 us; the launch traced here: 274 us
  waiting for transfers between devices  108 us (39%)
  blocking collectives  62.4 us (23%)
  matrix products  32 us (12%)
  between operations  30.9 us (11%)
  local copies, waits for them, and re-layouts  26.1 us (9%)
  other arithmetic  14.8 us (5%)
    all_gather x1, waiting for transfers between devices, body(): cols_near = lax.all_gather(col_low, 'row', axis=0, tiled=True)  80.5 us
    all_to_all x1, blocking collectives, sum_at_owner(): lax.all_to_all(split_up(array, dim, length), axis, 0, 0, tiled=True)  62.4 us
    dot_general x3, matrix products, tile_terms(): lax.dot_general(row_block, col_block, (((0,), (0,)), ((), ())), preferred...  19.3 us
    all_gather x1, waiting for transfers between devices, body(): rows_near = lax.all_gather(row_low, 'col', axis=0, tiled=True)  17.6 us
    unnamed x40, local copies, waits for them, and re-layouts  11.8 us
    unnamed x4, waiting for transfers between devices  10 us
    broadcast_in_dim x1, local copies, waits for them, and re-layouts, body(): jnp.zeros((row_count, emb_width, block_len), jnp.float32)  9.25 us
    sub x2, other arithmetic, adagrad(): return (weights - learn_rate * gradient / jnp.sqrt(grown), grown)  7.58 us
  transfers between devices with their start and end apart: 3, of which 3 were waited for; matrix products, arithmetic and copies ran while one was open for 7% of the time, Pallas kernels for 0%

commit v1 on v0

v1 whole, which is shorter than its diff:
```python
import jax
import jax.numpy as jnp
from jax import lax
from jax.experimental import pallas as pl
from jax.experimental.pallas import tpu as pltpu
from jax.sharding import PartitionSpec as P

err_scale = 0.03125
learn_rate = 0.1

DIM = 300
PAD = 304
HALF = 152
META = 160
BLOCK = 1024
LANES = 128
PARTS = 16
TILES = 3
COLS = 8
CHUNK = 256

f32 = jnp.float32
bf16 = jnp.bfloat16


def prep_kernel(wanted, row_ref, col_ref, low_ref, slice_ref):
    low_ref[0, 288:PAD, :] = jnp.zeros((16, BLOCK), bf16)
    low_ref[0, 0:DIM, :] = row_ref[0].astype(bf16)
    lane = lax.broadcasted_iota(jnp.int32, (8, LANES), 1)
    spot = lax.broadcasted_iota(jnp.int32, (8, LANES), 0)
    ask = [wanted[t] // COLS for t in range(TILES)]
    meta = jnp.where(lane == 0, ask[0], jnp.where(lane == 1, ask[1], ask[2])).astype(f32)
    for n in range(BLOCK // LANES):
        cut = slice(n * LANES, (n + 1) * LANES)
        top = jnp.concatenate([col_ref[0, 0:HALF, cut], meta], axis=0)
        slice_ref[2 * n] = top.astype(bf16)
        last = pltpu.roll(col_ref[0, DIM - 8 : DIM, cut], 4, 0)
        last = jnp.where(spot < 4, last, 0.0)
        low = jnp.concatenate([col_ref[0, HALF : DIM - 4, cut], last, meta], axis=0)
        slice_ref[2 * n + 1] = low.astype(bf16)


def prep(tile_cols, row_emb, col_emb):
    return pl.pallas_call(
        prep_kernel,
        out_shape=(
            jax.ShapeDtypeStruct((1, PAD, BLOCK), bf16),
            jax.ShapeDtypeStruct((PARTS, META, LANES), bf16),
        ),
        in_specs=[
            pl.BlockSpec(memory_space=pltpu.SMEM),
            pl.BlockSpec(memory_space=pltpu.VMEM),
            pl.BlockSpec(memory_space=pltpu.VMEM),
        ],
        name="prep",
    )(tile_cols, row_emb, col_emb)


def pick_kernel(held_ref, out_ref, meta_ref, asked, sem):
    for d in range(PARTS):
        meta_ref[d : d + 1, :] = held_ref[d, HALF:META, :].astype(f32)[0:1, :].astype(jnp.int32)
    move = pltpu.make_async_copy(meta_ref, asked, sem)
    move.start()
    move.wait()
    for d in range(PARTS):
        for t in range(TILES):
            out_ref[d, t] = held_ref[asked[d, t], 0:HALF, :]


def pick(held):
    return pl.pallas_call(
        pick_kernel,
        out_shape=(
            jax.ShapeDtypeStruct((PARTS, TILES, HALF, LANES), bf16),
            jax.ShapeDtypeStruct((PARTS, LANES), jnp.int32),
        ),
        in_specs=[pl.BlockSpec(memory_space=pltpu.VMEM)],
        scratch_shapes=[pltpu.SMEM((PARTS, LANES), jnp.int32), pltpu.SemaphoreType.DMA],
        name="pick",
    )(held)


def tile_kernel(
    rows, cols, part_ref, near_ref, count_ref, row_margin_ref, col_margin_ref,
    col_out_ref, row_out_ref, col_block, row_terms, col_term,
):
    t = pl.program_id(0)

    @pl.when(t == 0)
    def _():
        row_out_ref[...] = jnp.zeros((COLS, PAD, BLOCK), bf16)

    for s in range(PARTS):
        n, h = s // 2, s % 2
        col_block[h * HALF : (h + 1) * HALF, n * LANES : (n + 1) * LANES] = part_ref[s, 0]
    row_margin = jnp.transpose(row_margin_ref[0])
    col_margin = jnp.concatenate(
        [col_margin_ref[0, n : n + 1, :] for n in range(BLOCK // LANES)], axis=1
    )
    for c in range(BLOCK // CHUNK):
        cut = slice(c * CHUNK, (c + 1) * CHUNK)
        row_part = near_ref[0, :, cut]
        scores = lax.dot_general(
            row_part, col_block[...], (((0,), (0,)), ((), ())), preferred_element_type=f32
        )
        margin = jnp.concatenate(
            [row_margin[:, n : n + 1] for n in range(2 * c, 2 * c + 2)], axis=0
        )
        counted = count_ref[0, cut, :].astype(f32)
        capped = jnp.maximum(counted, 1.0)
        residue = scores - jnp.log(capped) + (margin + col_margin)
        weight = (0.1 * err_scale) + (0.25 * err_scale) * (counted * lax.rsqrt(capped))
        logistic = (0.5 * err_scale) + (0.5 * err_scale) * jnp.tanh(0.5 * residue)
        errors = jnp.where(counted > 0.0, weight * residue, logistic).astype(bf16)
        row_terms[t, :, cut] = lax.dot_general(
            col_block[...], errors, (((1,), (1,)), ((), ())), preferred_element_type=f32
        )
        term = jnp.dot(row_part, errors, preferred_element_type=f32)
        if c == 0:
            col_term[...] = term
        else:
            col_term[...] += term
    for s in range(PARTS):
        n, h = s // 2, s % 2
        col_out_ref[s, 0] = col_term[
            h * HALF : (h + 1) * HALF, n * LANES : (n + 1) * LANES
        ].astype(bf16)

    @pl.when(t == TILES - 1)
    def _():
        slots = [rows[k] % COLS for k in range(TILES)]
        for k in range(TILES):
            total = row_terms[k]
            for other in range(TILES):
                if other != k:
                    same = jnp.where(slots[other] == slots[k], 1.0, 0.0)
                    total = total + same * row_terms[other]
            row_out_ref[slots[k]] = total.astype(bf16)


def tile_terms(tile_rows, tile_cols, parts, near, counts, margins):
    grid_spec = pltpu.PrefetchScalarGridSpec(
        num_scalar_prefetch=2,
        grid=(TILES,),
        in_specs=[
            pl.BlockSpec((PARTS, 1, HALF, LANES), lambda t, rows, cols: (0, t, 0, 0)),
            pl.BlockSpec((1, PAD, BLOCK), lambda t, rows, cols: (rows[t] % COLS, 0, 0)),
            pl.BlockSpec((1, BLOCK, BLOCK), lambda t, rows, cols: (t, 0, 0)),
            pl.BlockSpec((1, 8, LANES), lambda t, rows, cols: (rows[t], 0, 0)),
            pl.BlockSpec((1, 8, LANES), lambda t, rows, cols: (cols[t], 0, 0)),
        ],
        out_specs=[
            pl.BlockSpec((PARTS, 1, HALF, LANES), lambda t, rows, cols: (0, t, 0, 0)),
            pl.BlockSpec((COLS, PAD, BLOCK), lambda t, rows, cols: (0, 0, 0)),
        ],
        scratch_shapes=[
            pltpu.VMEM((PAD, BLOCK), bf16),
            pltpu.VMEM((TILES, PAD, BLOCK), f32),
            pltpu.VMEM((PAD, BLOCK), f32),
        ],
    )
    return pl.pallas_call(
        tile_kernel,
        grid_spec=grid_spec,
        out_shape=(
            jax.ShapeDtypeStruct((PARTS, TILES, HALF, LANES), bf16),
            jax.ShapeDtypeStruct((COLS, PAD, BLOCK), bf16),
        ),
        compiler_params=pltpu.CompilerParams(
            dimension_semantics=("arbitrary",), vmem_limit_bytes=56 << 20
        ),
        name="tile_terms",
    )(tile_rows, tile_cols, parts, near, counts, margins, margins)


def owner_sum_kernel(asked, term_ref, out_ref, total):
    total[...] = jnp.zeros((PARTS, HALF, LANES), f32)
    for d in range(PARTS):
        for t in range(TILES):
            total[asked[d, t]] += term_ref[d, t].astype(f32)
    out_ref[...] = total[...].astype(bf16)


def owner_sum(asked, terms):
    return pl.pallas_call(
        owner_sum_kernel,
        out_shape=jax.ShapeDtypeStruct((PARTS, HALF, LANES), bf16),
        in_specs=[
            pl.BlockSpec(memory_space=pltpu.SMEM),
            pl.BlockSpec(memory_space=pltpu.VMEM),
        ],
        scratch_shapes=[pltpu.VMEM((PARTS, HALF, LANES), f32)],
        name="owner_sum",
    )(asked, terms)


def adagrad(weights, history, gradient):
    grown = history + gradient * gradient
    return (weights - learn_rate * gradient / jnp.sqrt(grown), grown)


def col_update_kernel(emb_ref, acc_ref, grad_ref, new_emb_ref, new_acc_ref):
    for n in range(BLOCK // LANES):
        cut = slice(n * LANES, (n + 1) * LANES)
        for h in range(2):
            length = HALF if h == 0 else DIM - HALF
            span = slice(h * HALF, h * HALF + length)
            new_emb_ref[0, span, cut], new_acc_ref[0, span, cut] = adagrad(
                emb_ref[0, span, cut],
                acc_ref[0, span, cut],
                grad_ref[2 * n + h].astype(f32)[0:length],
            )


def col_update(emb, acc, grad):
    shape = jax.ShapeDtypeStruct((1, DIM, BLOCK), f32)
    return pl.pallas_call(
        col_update_kernel,
        out_shape=(shape, shape),
        in_specs=[pl.BlockSpec(memory_space=pltpu.VMEM)] * 3,
        name="col_update",
    )(emb, acc, grad)


def body(row_emb, col_emb, row_acc, col_acc, marginal_log, tile_rows, tile_cols, counts):
    row_low, slices = prep(tile_cols, row_emb, col_emb)
    near = lax.all_gather(row_low, "col", axis=0, tiled=True)
    held = lax.all_to_all(slices, "row", 0, 0, tiled=True)
    picked, asked = pick(held)
    parts = lax.all_to_all(picked, "row", 0, 0, tiled=True)
    margins = marginal_log.reshape(-1, 8, LANES)
    col_terms, row_parts = tile_terms(tile_rows, tile_cols, parts, near, counts, margins)
    row_sum = lax.psum_scatter(row_parts, "col", scatter_dimension=0, tiled=True)
    terms = lax.all_to_all(col_terms, "row", 0, 0, tiled=True)
    sums = owner_sum(asked, terms)
    col_sum = lax.all_to_all(sums, "row", 0, 0, tiled=True)
    new_row_emb, new_row_acc = adagrad(row_emb, row_acc, row_sum[:, :DIM, :].astype(f32))
    new_col_emb, new_col_acc = col_update(col_emb, col_acc, col_sum)
    return (new_row_emb, new_col_emb, new_row_acc, new_col_acc)


def solution(mesh):
    block = P(("row", "col"), None, None)
    return jax.shard_map(
        body,
        mesh=mesh,
        in_specs=(block, block, block, block, P(), P(("row", "col")), P(("row", "col")), block),
        out_specs=(block, block, block, block),
        check_vma=False,
    )
```

time: 275 us -> 157 us (0.57)
  waiting for transfers between devices: 108 us -> 9.17 us
  Pallas kernels: 0 us -> 32.7 us
  matrix products: 32 us -> 0 us
  between operations: 30.9 us -> 14.1 us
  blocking collectives: 62.4 us -> 76.9 us
  other arithmetic: 14.8 us -> 1.76 us
  local copies, waits for them, and re-layouts: 26.1 us -> 18.2 us
  starting transfers between devices: 0.12 us -> 3.98 us
    all_gather x2 -> x1, waiting for transfers between devices: 98 us -> 0.01 us  [body(): near = lax.all_gather(row_low, 'col', axis=0, tiled=True)]
    pallas_call x0 -> x5, Pallas kernels: none -> 32.7 us  [the longest x1 19.9 us: tile_terms(): pl.pallas_call(tile_kernel, grid_spec=grid_spec, out_shape=(jax.ShapeDtyp...]
    dot_general x9 -> x0, matrix products: 32 us -> none  [the longest x3 19.3 us: tile_terms(): lax.dot_general(row_block, col_block, (((0,), (0,)), ((), ())), preferred...]
    all_to_all x1 -> x3, blocking collectives: 62.4 us -> 76.9 us  [the longest x1 29.5 us: body(): parts = lax.all_to_all(picked, 'row', 0, 0, tiled=True)]
    broadcast_in_dim x2 -> x0, local copies, waits for them, and re-layouts: 10.5 us -> none  [the longest x1 9.25 us: body(): jnp.zeros((row_count, emb_width, block_len), jnp.float32)]
    unnamed x4 -> x2, waiting for transfers between devices: 10 us -> 0.03 us
    all_to_all x0 -> x1, waiting for transfers between devices: none -> 9.14 us  [body(): col_sum = lax.all_to_all(sums, 'row', 0, 0, tiled=True)]
    unnamed x40 -> x19, local copies, waits for them, and re-layouts: 11.8 us -> 18.2 us
  transfers between devices with their start and end apart: 3 -> 3, of which waited for: 3 -> 1; matrix products, arithmetic and copies ran while one was open for 7% -> 5% of each run, Pallas kernels for 0% -> 6%
where the time goes in v1:
time: 157 us
  blocking collectives  76.9 us (49%)
  Pallas kernels  32.7 us (21%)
  local copies, waits for them, and re-layouts  18.2 us (12%)
  between operations  14.1 us (9%)
  waiting for transfers between devices  9.17 us (6%)
  starting transfers between devices  3.98 us (3%)
  other arithmetic  1.76 us (1%)
    all_to_all x1, blocking collectives, body(): parts = lax.all_to_all(picked, 'row', 0, 0, tiled=True)  29.5 us
    all_to_all x1, blocking collectives, body(): terms = lax.all_to_all(col_terms, 'row', 0, 0, tiled=True)  27.2 us
    all_to_all x1, blocking collectives, body(): held = lax.all_to_all(slices, 'row', 0, 0, tiled=True)  20.2 us
    pallas_call x1, Pallas kernels, tile_terms(): pl.pallas_call(tile_kernel, grid_spec=grid_spec, out_shape=(jax.ShapeDtyp...  19.9 us
    unnamed x19, local copies, waits for them, and re-layouts  18.2 us
    all_to_all x1, waiting for transfers between devices, body(): col_sum = lax.all_to_all(sums, 'row', 0, 0, tiled=True)  9.14 us
    all_to_all x1, starting transfers between devices, body(): col_sum = lax.all_to_all(sums, 'row', 0, 0, tiled=True)  3.9 us
    pallas_call x1, Pallas kernels, col_update(): pl.pallas_call(col_update_kernel, out_shape=(shape, shape), in_specs=[pl....  3.88 us
  transfers between devices with their start and end apart: 3, of which 1 were waited for; matrix products, arithmetic and copies ran while one was open for 5% of the time, Pallas kernels for 6%

profile of v1, /device:TPU:0, one launch (start us, length us, event | category | flops | bytes accessed | tf_op | source)
XLA Modules:
  0.0 156.7 jit_solution(11691694396321185950)
XLA Ops:
  7.2 0.0 copy-start
  7.2 0.0 all-gather.2.cloned.1.call-start
  7.2 2.7 %copy.23.col_ref.emb_ref = f32[1,300,1024]{2,1,0:T(8,128)} copy(f32[1,300,1024]{2,0,1:T(1,128)} %param.9) | data formatting | bytes 2457600 | tf_op args[1]
  9.9 0.0 copy-done
  9.9 1.3 copy.25.row_ref
  11.2 2.8 %prep.1 = (bf16[1,304,1024]{2,1,0:T(8,128)(2,1)}, bf16[16,160,128]{2,1,0:T(8,128)(2,1)}) custom-call(s32[3]{0:T(128)} %cols.1, f32[1,300,1024]{2,1,0:T(8,128)} %copy.25.row_ref, f32[1,300,1024]{2,1,0:T(8,128)} %copy.23.col_ref.emb_ref), custom_call_target="tpu_custom_call" | custom-call | tf_op jit(solution)/shard_map/prep/pallas_call | solution.py:44
  14.0 0.0 all-gather.2.cloned.1.call-update
  14.0 0.0 reduce-scatter.2.cloned.1.call-start
  14.1 20.2 %all_to_all.20.held_ref = bf16[16,160,128]{2,1,0:T(8,128)(2,1)} all-to-all(bf16[16,160,128]{2,1,0:T(8,128)(2,1)} %get-tuple-element.12), channel_id=1, replica_groups=mesh['row'=16,'col'=8] {'row'}, dimensions={0} | all-to-all | bytes 1310720 | tf_op jit(solution)/shard_map/all_to_all | solution.py:228
  34.3 3.2 %pick.1 = (bf16[16,3,152,128]{3,2,1,0:T(8,128)(2,1)}, s32[16,128]{1,0:T(8,128)}) custom-call(bf16[16,160,128]{2,1,0:T(8,128)(2,1)} %all_to_all.20.held_ref), custom_call_target="tpu_custom_call" | custom-call | tf_op jit(solution)/shard_map/pick/pallas_call | solution.py:71
  37.4 29.5 %all_to_all.21.part_ref = bf16[16,3,152,128]{3,2,1,0:T(8,128)(2,1)} all-to-all(bf16[16,3,152,128]{3,2,1,0:T(8,128)(2,1)} %get-tuple-element.13), channel_id=1, replica_groups=mesh['row'=16,'col'=8] {'row'}, dimensions={0} | all-to-all | bytes 3735552 | tf_op jit(solution)/shard_map/all_to_all | solution.py:230
  66.9 0.0 all-gather.2.cloned.1.call-done.near_ref
  66.9 19.9 %tile_terms.1 = (bf16[16,3,152,128]{3,2,1,0:T(8,128)(2,1)}, bf16[8,304,1024]{2,1,0:T(8,128)(2,1)}) custom-call(s32[3]{0:T(128)} %rows.1, s32[3]{0:T(128)} %cols.1, bf16[16,3,152,128]{3,2,1,0:T(8,128)(2,1)} %all_to_all.21.part_ref, bf16[8,304,1024]{2,1,0:T(8,128)(2,1)} %all-gather.2.cloned.1.call-done.near_ref, s32[3,1024,1024]{2,1,0:T(8,128)} %count_ref.1, ...), custom_call_target="tpu_custom_call" | custom-call | tf_op jit(solution)/shard_map/tile_terms/pallas_call | solution.py:162
  86.8 0.0 copy-start.2
  86.8 0.0 reduce-scatter.2.cloned.1.call-update
  86.8 1.5 copy-done.2
  88.3 27.2 %all_to_all.22.term_ref = bf16[16,3,152,128]{3,2,1,0:T(8,128)(2,1)} all-to-all(bf16[16,3,152,128]{3,2,1,0:T(8,128)(2,1)S(1)} %copy-done.2), channel_id=1, replica_groups=mesh['row'=16,'col'=8] {'row'}, dimensions={0} | all-to-all | bytes 3735552 | tf_op jit(solution)/shard_map/all_to_all | solution.py:234
  115.5 3.0 %owner_sum.1 = bf16[16,152,128]{2,1,0:T(8,128)(2,1)} custom-call(s32[16,128]{1,0:T(8,128)} %get-tuple-element.16.asked, bf16[16,3,152,128]{3,2,1,0:T(8,128)(2,1)} %all_to_all.22.term_ref), custom_call_target="tpu_custom_call" | custom-call | tf_op jit(solution)/shard_map/owner_sum/pallas_call | solution.py:185
  118.5 0.0 copy-start.4
  118.5 3.9 %all-to-all-start.3 = ((bf16[16,152,128]{2,1,0:T(8,128)(2,1)}), bf16[16,152,128]{2,1,0:T(8,128)(2,1)S(1)}, u32[]{:S(2)}, u32[]{:S(2)}) async-start(bf16[16,152,128]{2,1,0:T(8,128)(2,1)} %owner_sum.1), calls=%async_computation.4 | async-start | bytes 1245184 | tf_op jit(solution)/shard_map/all_to_all | solution.py:236
  122.4 0.0 copy-done.4
  122.4 1.3 copy.27.acc_ref
  123.7 9.1 %all-to-all-done.3.grad_ref = bf16[16,152,128]{2,1,0:T(8,128)(2,1)S(1)} async-done(((bf16[16,152,128]{2,1,0:T(8,128)(2,1)}), bf16[16,152,128]{2,1,0:T(8,128)(2,1)S(1)}, u32[]{:S(2)}, u32[]{:S(2)}) %all-to-all-start.3) | async-done | bytes 622624 | tf_op jit(solution)/shard_map/all_to_all | solution.py:236
  132.8 0.8 copy-done.1
  133.7 3.9 %col_update.1 = (f32[1,300,1024]{2,1,0:T(8,128)}, f32[1,300,1024]{2,1,0:T(8,128)}) custom-call(f32[1,300,1024]{2,1,0:T(8,128)} %copy.23.col_ref.emb_ref, f32[1,300,1024]{2,1,0:T(8,128)} %copy.27.acc_ref, bf16[16,152,128]{2,1,0:T(8,128)(2,1)} %copy-done.1), custom_call_target="tpu_custom_call" | custom-call | tf_op jit(solution)/shard_map/col_update/pallas_call | solution.py:217
  137.5 3.7 %copy.29 = f32[1,300,1024]{2,0,1:T(1,128)} copy(f32[1,300,1024]{2,1,0:T(8,128)} %get-tuple-element.25) | data formatting | bytes 2457600
  141.2 0.0 copy-done.3
  141.2 2.3 %copy.31 = f32[1,300,1024]{2,0,1:T(1,128)} copy(f32[1,300,1024]{2,1,0:T(8,128)S(1)} %copy-done.3) | data formatting | bytes 2457600
  143.5 0.0 copy-done.5
  143.5 1.8 %fusion.1 = (f32[1,300,1024]{2,1,0:T(8,128)S(1)}, f32[1,300,1024]{2,1,0:T(8,128)S(1)}) fusion(bf16[1,304,1024]{2,1,0:T(8,128)(2,1)} %reduce-scatter.2.cloned.1.call-done, f32[1,300,1024]{2,0,1:T(1,128)S(1)} %copy-done, f32[1,300,1024]{2,0,1:T(1,128)S(1)} %copy-done.5), kind=kLoop, calls=%fused_computation.3 | loop fusion | flops 1843200 | bytes 5529600 | tf_op jit(solution)/shard_map/sub | solution.py:199
  145.3 2.3 %copy.28 = f32[1,300,1024]{2,0,1:T(1,128)} copy(f32[1,300,1024]{2,1,0:T(8,128)S(1)} %get-tuple-element.28) | data formatting | bytes 2457600
  147.6 2.3 %copy.30 = f32[1,300,1024]{2,0,1:T(1,128)} copy(f32[1,300,1024]{2,1,0:T(8,128)S(1)} %get-tuple-element.29) | data formatting | bytes 2457600
  (4 shorter events, 0.0 us)
Async XLA Ops:
  7.2 2.7 %copy-start = (f32[1,300,1024]{2,0,1:T(1,128)S(1)}, f32[1,300,1024]{2,0,1:T(1,128)}, u32[]{:S(2)}) copy-start(f32[1,300,1024]{2,0,1:T(1,128)} %param.8) | copy-start | bytes 3686404
  7.2 59.8 %all-gather.2.cloned.1.call-start = ((), (), s32[]{:S(2)}) async-start(), calls=%async_computation.5 | async-start | bytes 5603328 | tf_op jit(solution)/shard_map/all_gather | solution.py:227
  14.0 129.5 %reduce-scatter.2.cloned.1.call-start = ((), (), s32[]{:S(2)}) async-start(), calls=%async_computation.6 | async-start | bytes 5603328 | tf_op jit(solution)/shard_map/reduce_scatter | solution.py:233
  86.8 1.5 copy-start.2
  118.5 3.9 %copy-start.4 = (f32[1,300,1024]{2,0,1:T(1,128)S(1)}, f32[1,300,1024]{2,0,1:T(1,128)}, u32[]{:S(2)}) copy-start(f32[1,300,1024]{2,0,1:T(1,128)} %param.11) | copy-start | bytes 3686404
  118.5 14.4 %all-to-all-start.3 = ((bf16[16,152,128]{2,1,0:T(8,128)(2,1)}), bf16[16,152,128]{2,1,0:T(8,128)(2,1)S(1)}, u32[]{:S(2)}, u32[]{:S(2)}) async-start(bf16[16,152,128]{2,1,0:T(8,128)(2,1)} %owner_sum.1), calls=%async_computation.4 | async-start | bytes 1245184 | tf_op jit(solution)/shard_map/all_to_all | solution.py:236
  132.8 0.8 copy-start.1
  137.5 3.7 %copy-start.3 = (f32[1,300,1024]{2,1,0:T(8,128)S(1)}, f32[1,300,1024]{2,1,0:T(8,128)}, u32[]{:S(2)}) copy-start(f32[1,300,1024]{2,1,0:T(8,128)} %get-tuple-element.27) | copy-start | bytes 3686404
  141.2 2.3 %copy-start.5 = (f32[1,300,1024]{2,0,1:T(1,128)S(1)}, f32[1,300,1024]{2,0,1:T(1,128)}, u32[]{:S(2)}) copy-start(f32[1,300,1024]{2,0,1:T(1,128)} %param.10) | copy-start | bytes 3686404
Sparse Core Ops, SparseCore 0:
  14.1 38.0 all-gather.1
  86.9 38.6 reduce-scatter.1

commit v2 on v1

v2 whole, which is shorter than its diff:
```python
import jax
import jax.numpy as jnp
from jax import lax
from jax.experimental import pallas as pl
from jax.experimental.pallas import tpu as pltpu
from jax.sharding import PartitionSpec as P


err_scale = 0.03125
learn_rate = 0.1

DIM = 300
PAD = 304
HALF = 152
META = 160
BLOCK = 1024
LANES = 128
PARTS = 16
TILES = 3
COLS = 8
FIRST = 512
GROUPS = 8

f32 = jnp.float32
bf16 = jnp.bfloat16

SMEM = pl.BlockSpec(memory_space=pltpu.SMEM)
VMEM = pl.BlockSpec(memory_space=pltpu.VMEM)
HBM = pl.BlockSpec(memory_space=pl.ANY)


def span(first, length, n):
    return pl.ds(first * GROUPS + n, length, stride=GROUPS)


def cut_kernel(wanted, col_ref, slice_ref, col, sems):
    edge = HALF * GROUPS
    moves = [
        pltpu.make_async_copy(col_ref.at[:edge], col.at[:edge], sems.at[0]),
        pltpu.make_async_copy(col_ref.at[edge:], col.at[edge:], sems.at[1]),
    ]
    for move in moves:
        move.start()
    lane = lax.broadcasted_iota(jnp.int32, (8, LANES), 1)
    spot = lax.broadcasted_iota(jnp.int32, (8, LANES), 0)
    ask = [wanted[t] // COLS for t in range(TILES)]
    meta = jnp.where(lane == 0, ask[0], jnp.where(lane == 1, ask[1], ask[2])).astype(f32)
    moves[0].wait()
    for n in range(GROUPS):
        top = jnp.concatenate([col[span(0, HALF, n), :], meta], axis=0)
        slice_ref[2 * n] = top.astype(bf16)
    moves[1].wait()
    for n in range(GROUPS):
        last = pltpu.roll(col[span(DIM - 8, 8, n), :], 4, 0)
        last = jnp.where(spot < 4, last, 0.0)
        low = jnp.concatenate([col[span(HALF, DIM - 4 - HALF, n), :], last, meta], axis=0)
        slice_ref[2 * n + 1] = low.astype(bf16)


def cut_up(tile_cols, col_emb):
    return pl.pallas_call(
        cut_kernel,
        out_shape=jax.ShapeDtypeStruct((PARTS, META, LANES), bf16),
        in_specs=[SMEM, HBM],
        out_specs=VMEM,
        scratch_shapes=[pltpu.VMEM((DIM * GROUPS, LANES), f32), pltpu.SemaphoreType.DMA((2,))],
        compiler_params=pltpu.CompilerParams(vmem_limit_bytes=8 << 20),
        name="cut_up",
    )(tile_cols, col_emb)


def low_kernel(row_ref, low_ref):
    low_ref[0, 288:PAD, :] = jnp.zeros((16, BLOCK), bf16)
    for n in range(GROUPS):
        low_ref[0, 0:DIM, n * LANES : (n + 1) * LANES] = row_ref[span(0, DIM, n), :].astype(bf16)


def lower(row_emb):
    return pl.pallas_call(
        low_kernel,
        out_shape=jax.ShapeDtypeStruct((1, PAD, BLOCK), bf16),
        in_specs=[VMEM],
        out_specs=VMEM,
        compiler_params=pltpu.CompilerParams(vmem_limit_bytes=8 << 20),
        name="lower",
    )(row_emb)


def pick_kernel(held_ref, out_ref, meta_ref, picked, asked, sem, sems):
    for d in range(PARTS):
        meta_ref[d : d + 1, :] = held_ref[d, HALF:META, :].astype(f32)[0:1, :].astype(jnp.int32)
    move = pltpu.make_async_copy(meta_ref, asked, sem)
    move.start()
    move.wait()
    quarter = PARTS // 4
    moves = []
    for q in range(4):
        some = pl.ds(q * quarter, quarter)
        for d in range(q * quarter, (q + 1) * quarter):
            for t in range(TILES):
                picked[d, t] = held_ref[asked[d, t], 0:HALF, :]
        moves.append(pltpu.make_async_copy(picked.at[some], out_ref.at[some], sems.at[q]))
        moves[q].start()
    for move in moves:
        move.wait()


def pick(held):
    return pl.pallas_call(
        pick_kernel,
        out_shape=(
            pltpu.HBM((PARTS, TILES, HALF, LANES), bf16),
            jax.ShapeDtypeStruct((PARTS, LANES), jnp.int32),
        ),
        in_specs=[VMEM],
        out_specs=[HBM, VMEM],
        scratch_shapes=[
            pltpu.VMEM((PARTS, TILES, HALF, LANES), bf16),
            pltpu.SMEM((PARTS, LANES), jnp.int32),
            pltpu.SemaphoreType.DMA,
            pltpu.SemaphoreType.DMA((4,)),
        ],
        compiler_params=pltpu.CompilerParams(vmem_limit_bytes=8 << 20),
        name="pick",
    )(held)


def ready_kernel(
    rows, cols, count_ref, margin_ref, weight_ref, offset_ref, blank_ref, other_blank_ref,
    margin, zero, sems,
):
    t = pl.program_id(0)

    def margin_moves(k):
        return [
            pltpu.make_async_copy(margin_ref.at[rows[k]], margin.at[k, 0], sems.at[2 * k]),
            pltpu.make_async_copy(margin_ref.at[cols[k]], margin.at[k, 1], sems.at[2 * k + 1]),
        ]

    blank_moves = [
        pltpu.make_async_copy(zero, ref.at[s], sems.at[2 * TILES + 4 * i + s])
        for i, ref in enumerate((blank_ref, other_blank_ref))
        for s in range(4)
    ]

    @pl.when(t == 0)
    def _():
        for k in range(TILES):
            for move in margin_moves(k):
                move.start()
        zero[...] = jnp.zeros((PAD, BLOCK), bf16)
        for move in blank_moves:
            move.start()

    for move in margin_moves(t):
        move.wait()
    row_margin = jnp.transpose(margin[t, 0])
    col_margin = jnp.concatenate([margin[t, 1, n : n + 1, :] for n in range(GROUPS)], axis=1)
    for n in range(GROUPS):
        cut = slice(n * LANES, (n + 1) * LANES)
        counted = count_ref[0, cut, :].astype(f32)
        capped = jnp.maximum(counted, 1.0)
        offset_ref[0, cut, :] = (row_margin[:, n : n + 1] + col_margin) - jnp.log(capped)
        weight = (0.1 * err_scale) + (0.25 * err_scale) * (counted * lax.rsqrt(capped))
        weight_ref[0, cut, :] = jnp.where(counted > 0.0, weight, 0.0)

    @pl.when(t == TILES - 1)
    def _():
        for move in blank_moves:
            move.wait()


def ready(tile_rows, tile_cols, counts, margins):
    square = pl.BlockSpec((1, BLOCK, BLOCK), lambda t, *_: (t, 0, 0))
    grid_spec = pltpu.PrefetchScalarGridSpec(
        num_scalar_prefetch=2,
        grid=(TILES,),
        in_specs=[square, HBM],
        out_specs=[square, square, HBM, HBM],
        scratch_shapes=[
            pltpu.VMEM((TILES, 2, GROUPS, LANES), f32),
            pltpu.VMEM((PAD, BLOCK), bf16),
            pltpu.SemaphoreType.DMA((2 * TILES + 8,)),
        ],
    )
    return pl.pallas_call(
        ready_kernel,
        grid_spec=grid_spec,
        out_shape=(
            jax.ShapeDtypeStruct((TILES, BLOCK, BLOCK), f32),
            jax.ShapeDtypeStruct((TILES, BLOCK, BLOCK), f32),
            pltpu.HBM((4, PAD, BLOCK), bf16),
            pltpu.HBM((4, PAD, BLOCK), bf16),
        ),
        compiler_params=pltpu.CompilerParams(
            dimension_semantics=("arbitrary",), vmem_limit_bytes=48 << 20
        ),
        name="ready",
    )(tile_rows, tile_cols, counts, margins)


def tile_kernel(
    place, rows, part_ref, same_ref, other_ref, weight_ref, offset_ref, blank_ref, other_blank_ref,
    col_out_ref, keep_ref, give_ref,
    part, near, weights, offsets, col_block, row_terms, whole, col_out, sems, out_sems,
):
    slots = [rows[k] % COLS for k in range(TILES)]
    own = [slots[k] % 2 == place[0] % 2 for k in range(TILES)]
    fetch = [lax.rem(place[0] // 2 - slots[k] // 2 + 4, 4) for k in range(TILES)]
    leave = [lax.rem(slots[k] // 2 - place[0] // 2 + 4, 4) for k in range(TILES)]

    def near_move(k, ref=same_ref):
        return pltpu.make_async_copy(ref.at[fetch[k]], near.at[k], sems.at[k, 0])

    def part_move(k):
        return pltpu.make_async_copy(part_ref.at[:, k], part.at[k], sems.at[k, 1])

    def moves(k, c, width):
        cut = pl.ds(c * width, width)
        return [
            pltpu.make_async_copy(weight_ref.at[k, cut, :], weights.at[k, cut, :], sems.at[k, 2 + c]),
            pltpu.make_async_copy(offset_ref.at[k, cut, :], offsets.at[k, cut, :], sems.at[k, 4 + c]),
        ]

    def out_move(k):
        return pltpu.make_async_copy(col_out.at[k], col_out_ref.at[:, k], out_sems.at[k])

    widths = [FIRST] + [BLOCK] * (TILES - 1)
    for k in range(TILES):
        part_move(k).start()
        pl.when(own[k])(near_move(k).start)
        pl.when(jnp.logical_not(own[k]))(near_move(k, other_ref).start)
        for c in range(BLOCK // widths[k]):
            for move in moves(k, c, widths[k]):
                move.start()

    for t in range(TILES):
        part_move(t).wait()
        for s in range(PARTS):
            n, h = s // 2, s % 2
            col_block[t, h * HALF : (h + 1) * HALF, n * LANES : (n + 1) * LANES] = part[t, s]
        near_move(t).wait()
        term = None
        for c in range(BLOCK // widths[t]):
            cut = slice(c * widths[t], (c + 1) * widths[t])
            row_part = near[t, :, cut]
            scores = lax.dot_general(
                row_part, col_block[t], (((0,), (0,)), ((), ())), preferred_element_type=f32
            )
            for move in moves(t, c, widths[t]):
                move.wait()
            weight = weights[t, cut, :]
            residue = scores + offsets[t, cut, :]
            logistic = (0.5 * err_scale) + (0.5 * err_scale) * jnp.tanh(0.5 * residue)
            errors = jnp.where(weight > 0.0, weight * residue, logistic).astype(bf16)
            row_terms[t, :, cut] = lax.dot_general(
                col_block[t], errors, (((1,), (1,)), ((), ())), preferred_element_type=f32
            )
            piece = jnp.dot(row_part, errors, preferred_element_type=f32)
            term = piece if term is None else term + piece
        term = term.astype(bf16)
        for s in range(PARTS):
            n, h = s // 2, s % 2
            col_out[t, s] = term[h * HALF : (h + 1) * HALF, n * LANES : (n + 1) * LANES]
        out_move(t).start()

    fresh = [slots[0] >= 0, slots[1] != slots[0], (slots[2] != slots[0]) & (slots[2] != slots[1])]

    def sum_move(k, ref):
        return pltpu.make_async_copy(whole.at[k], ref.at[leave[k]], out_sems.at[TILES + k])

    for k in range(TILES):
        total = row_terms[k]
        for other in range(k + 1, TILES):
            same = jnp.where(slots[other] == slots[k], 1.0, 0.0)
            total = total + same * row_terms[other]
        whole[k] = total.astype(bf16)
    for k in range(TILES):
        pl.when(fresh[k] & own[k])(sum_move(k, keep_ref).start)
        pl.when(fresh[k] & jnp.logical_not(own[k]))(sum_move(k, give_ref).start)
    for k in range(TILES):
        pl.when(fresh[k])(sum_move(k, keep_ref).wait)
        out_move(k).wait()


def tile_terms(place, tile_rows, parts, same, other, weight, offset, blank, other_blank):
    quad = pltpu.HBM((4, PAD, BLOCK), bf16)
    return pl.pallas_call(
        tile_kernel,
        in_specs=[SMEM, SMEM] + [HBM] * 7,
        out_specs=[HBM] * 3,
        scratch_shapes=[
            pltpu.VMEM((TILES, PARTS, HALF, LANES), bf16),
            pltpu.VMEM((TILES, PAD, BLOCK), bf16),
            pltpu.VMEM((TILES, BLOCK, BLOCK), f32),
            pltpu.VMEM((TILES, BLOCK, BLOCK), f32),
            pltpu.VMEM((TILES, PAD, BLOCK), bf16),
            pltpu.VMEM((TILES, PAD, BLOCK), f32),
            pltpu.VMEM((TILES, PAD, BLOCK), bf16),
            pltpu.VMEM((TILES, PARTS, HALF, LANES), bf16),
            pltpu.SemaphoreType.DMA((TILES, 6)),
            pltpu.SemaphoreType.DMA((2 * TILES,)),
        ],
        out_shape=(pltpu.HBM((PARTS, TILES, HALF, LANES), bf16), quad, quad),
        input_output_aliases={7: 1, 8: 2},
        compiler_params=pltpu.CompilerParams(vmem_limit_bytes=60 << 20),
        name="tile_terms",
    )(place, tile_rows, parts, same, other, weight, offset, blank, other_blank)


def join_kernel(keep_ref, got_ref, *out_refs):
    for k in range(4):
        out_refs[k][...] = (keep_ref[k].astype(f32) + got_ref[k].astype(f32)).astype(bf16)


def join(keep, got):
    return pl.pallas_call(
        join_kernel,
        out_shape=[jax.ShapeDtypeStruct((PAD, BLOCK), bf16)] * 4,
        in_specs=[VMEM] * 2,
        compiler_params=pltpu.CompilerParams(vmem_limit_bytes=16 << 20),
        name="join",
    )(keep, got)


def owner_sum_kernel(asked, term_ref, out_ref, total):
    total[...] = jnp.zeros((PARTS, HALF, LANES), f32)
    for d in range(PARTS):
        for t in range(TILES):
            total[asked[d, t]] += term_ref[d, t].astype(f32)
    out_ref[...] = total[...].astype(bf16)


def owner_sum(asked, terms):
    return pl.pallas_call(
        owner_sum_kernel,
        out_shape=jax.ShapeDtypeStruct((PARTS, HALF, LANES), bf16),
        in_specs=[SMEM, VMEM],
        out_specs=VMEM,
        scratch_shapes=[pltpu.VMEM((PARTS, HALF, LANES), f32)],
        compiler_params=pltpu.CompilerParams(vmem_limit_bytes=12 << 20),
        name="owner_sum",
    )(asked, terms)


def adagrad(weights, history, gradient):
    grown = history + gradient * gradient
    return (weights - learn_rate * gradient / jnp.sqrt(grown), grown)


def col_update_kernel(emb_ref, acc_ref, grad_ref, new_emb_ref, new_acc_ref, held, new, sems, out_sems):
    edge = HALF * GROUPS
    cuts = [pl.ds(0, edge), pl.ds(edge, DIM * GROUPS - edge)]
    for h in range(2):
        for i, ref in enumerate((emb_ref, acc_ref)):
            pltpu.make_async_copy(ref.at[cuts[h]], held.at[i, cuts[h]], sems.at[i, h]).start()
    for h in range(2):
        for i, ref in enumerate((emb_ref, acc_ref)):
            pltpu.make_async_copy(ref.at[cuts[h]], held.at[i, cuts[h]], sems.at[i, h]).wait()
        length = HALF if h == 0 else DIM - HALF
        for n in range(GROUPS):
            rows = span(h * HALF, length, n)
            new[0, rows, :], new[1, rows, :] = adagrad(
                held[0, rows, :], held[1, rows, :], grad_ref[2 * n + h].astype(f32)[0:length]
            )
        for i, ref in enumerate((new_emb_ref, new_acc_ref)):
            pltpu.make_async_copy(new.at[i, cuts[h]], ref.at[cuts[h]], out_sems.at[i, h]).start()
    for h in range(2):
        for i, ref in enumerate((new_emb_ref, new_acc_ref)):
            pltpu.make_async_copy(new.at[i, cuts[h]], ref.at[cuts[h]], out_sems.at[i, h]).wait()


def col_update(emb, acc, grad):
    shape = jax.ShapeDtypeStruct((GROUPS * DIM, LANES), f32)
    new_emb, new_acc = pl.pallas_call(
        col_update_kernel,
        out_shape=(shape, shape),
        in_specs=[HBM, HBM, VMEM],
        out_specs=[HBM, HBM],
        scratch_shapes=[
            pltpu.VMEM((2, GROUPS * DIM, LANES), f32),
            pltpu.VMEM((2, GROUPS * DIM, LANES), f32),
            pltpu.SemaphoreType.DMA((2, 2)),
            pltpu.SemaphoreType.DMA((2, 2)),
        ],
        compiler_params=pltpu.CompilerParams(vmem_limit_bytes=12 << 20),
        name="col_update",
    )(emb, acc, grad)
    return new_emb.reshape(1, DIM, BLOCK), new_acc.reshape(1, DIM, BLOCK)


def row_update_kernel(emb_ref, acc_ref, *refs):
    grad_refs, (new_emb_ref, new_acc_ref) = refs[:4], refs[4:]
    for n in range(GROUPS):
        rows = span(0, DIM, n)
        cut = slice(n * LANES, (n + 1) * LANES)
        first, *others = [ref[:, cut].astype(f32)[0:DIM] for ref in grad_refs]
        grad = (first + others[0]) + (others[1] + others[2])
        new_emb_ref[rows, :], new_acc_ref[rows, :] = adagrad(emb_ref[rows, :], acc_ref[rows, :], grad)


def row_update(emb, acc, grads):
    shape = jax.ShapeDtypeStruct((GROUPS * DIM, LANES), f32)
    new_emb, new_acc = pl.pallas_call(
        row_update_kernel,
        out_shape=(shape, shape),
        in_specs=[VMEM] * 6,
        compiler_params=pltpu.CompilerParams(vmem_limit_bytes=16 << 20),
        name="row_update",
    )(emb, acc, *grads)
    return new_emb.reshape(1, DIM, BLOCK), new_acc.reshape(1, DIM, BLOCK)


def send_along_z(array, step):
    return lax.ppermute(array, "col", [(i, (i + 2 * step) % COLS) for i in range(COLS)])


def swap_cores(array):
    return lax.ppermute(array, "col", [(i, i ^ 1) for i in range(COLS)])


def body(row_emb, col_emb, row_acc, col_acc, marginal_log, tile_rows, tile_cols, counts):
    row_emb, col_emb, row_acc, col_acc = (
        array.reshape(GROUPS * DIM, LANES) for array in (row_emb, col_emb, row_acc, col_acc)
    )
    margins = marginal_log.reshape(-1, GROUPS, LANES)
    place = lax.axis_index("col").astype(jnp.int32).reshape(1)
    slices = cut_up(tile_cols, col_emb)
    row_low = lower(row_emb)
    held = lax.all_to_all(slices, "row", 0, 0, tiled=True)
    near = [row_low] + [send_along_z(row_low, step) for step in (1, 2, 3)]
    weight, offset, blank, other_blank = ready(tile_rows, tile_cols, counts, margins)
    picked, asked = pick(held)
    parts = lax.all_to_all(picked, "row", 0, 0, tiled=True)
    same = jnp.concatenate(near, axis=0)
    other = swap_cores(same)
    terms, keep, give = tile_terms(
        place, tile_rows, parts, same, other, weight, offset, blank, other_blank
    )
    got = swap_cores(give)
    terms = lax.all_to_all(terms, "row", 0, 0, tiled=True)
    grads = join(keep, got)
    grads = [grads[0]] + [send_along_z(grads[step], step) for step in (1, 2, 3)]
    sums = owner_sum(asked, terms)
    col_sum = lax.all_to_all(sums, "row", 0, 0, tiled=True)
    new_row_emb, new_row_acc = row_update(row_emb, row_acc, grads)
    new_col_emb, new_col_acc = col_update(col_emb, col_acc, col_sum)
    return (new_row_emb, new_col_emb, new_row_acc, new_col_acc)


def solution(mesh):
    block = P(("row", "col"), None, None)
    return jax.shard_map(
        body,
        mesh=mesh,
        in_specs=(block, block, block, block, P(), P(("row", "col")), P(("row", "col")), block),
        out_specs=(block, block, block, block),
        check_vma=False,
    )
```

time: 157 us -> 169 us (1.076)
  waiting for transfers between devices: 9.17 us -> 66.7 us
  blocking collectives: 76.9 us -> 35.9 us
  local copies, waits for them, and re-layouts: 18.2 us -> 1.33 us
  starting transfers between devices: 3.98 us -> 18.1 us
  between operations: 14.1 us -> 0.87 us
  Pallas kernels: 32.7 us -> 45.2 us
    all_to_all x2 -> x1, blocking collectives: 56.7 us -> 15.4 us  [body(): col_sum = lax.all_to_all(sums, 'row', 0, 0, tiled=True)]
    ppermute x0 -> x8, waiting for transfers between devices: none -> 29.3 us  [the longest x6 28.8 us: send_along_z(): lax.ppermute(array, 'col', [(i, (i + 2 * step) % COLS) for i in range(COL...]
    all_to_all x1 -> x2, waiting for transfers between devices: 9.14 us -> 37.4 us  [the longest x1 24.5 us: body(): terms = lax.all_to_all(terms, 'row', 0, 0, tiled=True)]
    unnamed x19 -> x22, local copies, waits for them, and re-layouts: 18.2 us -> 1.33 us
    pallas_call x4 -> x8, Pallas kernels: 29.7 us -> 43.2 us  [the longest x1 15.3 us: tile_terms(): pl.pallas_call(tile_kernel, in_specs=[SMEM, SMEM] + [HBM] * 7, out_specs=...]
    ppermute x0 -> x8, starting transfers between devices: none -> 8.89 us  [the longest x6 8.71 us: send_along_z(): lax.ppermute(array, 'col', [(i, (i + 2 * step) % COLS) for i in range(COL...]
    all_to_all x1 -> x2, starting transfers between devices: 3.9 us -> 9.18 us  [the longest x1 4.61 us: body(): parts = lax.all_to_all(picked, 'row', 0, 0, tiled=True)]
    sub x1 -> x0, other arithmetic: 1.76 us -> none  [adagrad(): return (weights - learn_rate * gradient / jnp.sqrt(grown), grown)]
  transfers between devices with their start and end apart: 3 -> 10, of which waited for: 1 -> 5; matrix products, arithmetic and copies ran while one was open for 5% -> 0% of each run, Pallas kernels for 6% -> 15%
where the time goes in v2:
time: 169 us; the launch traced here: 168 us
  waiting for transfers between devices  66.7 us (39%)
  Pallas kernels  45.2 us (27%)
  blocking collectives  35.9 us (21%)
  starting transfers between devices  18.1 us (11%)
    ppermute x6, waiting for transfers between devices, send_along_z(): lax.ppermute(array, 'col', [(i, (i + 2 * step) % COLS) for i in range(COL...  28.8 us
    all_to_all x1, waiting for transfers between devices, body(): terms = lax.all_to_all(terms, 'row', 0, 0, tiled=True)  24.5 us
    all_to_all x1, blocking collectives, body(): held = lax.all_to_all(slices, 'row', 0, 0, tiled=True)  20.4 us
    all_to_all x1, blocking collectives, body(): col_sum = lax.all_to_all(sums, 'row', 0, 0, tiled=True)  15.4 us
    pallas_call x1, Pallas kernels, tile_terms(): pl.pallas_call(tile_kernel, in_specs=[SMEM, SMEM] + [HBM] * 7, out_specs=...  15.3 us
    pallas_call x1, Pallas kernels, ready(): pl.pallas_call(ready_kernel, grid_spec=grid_spec, out_shape=(jax.ShapeDty...  14.8 us
    all_to_all x1, waiting for transfers between devices, body(): parts = lax.all_to_all(picked, 'row', 0, 0, tiled=True)  12.9 us
    ppermute x6, starting transfers between devices, send_along_z(): lax.ppermute(array, 'col', [(i, (i + 2 * step) % COLS) for i in range(COL...  8.71 us
  transfers between devices with their start and end apart: 10, of which 5 were waited for; matrix products, arithmetic and copies ran while one was open for 0% of the time, Pallas kernels for 15%

profile of v2, /device:TPU:0, one launch (start us, length us, event | category | flops | bytes accessed | tf_op | source)
XLA Modules:
  0.0 168.3 jit_solution(17376582910780444031)
XLA Ops:
  0.6 0.0 copy-start.1
  0.6 1.3 copy-done.1
  1.9 0.3 lower.1
  2.2 0.0 copy-start.3
  2.2 0.0 copy-start.9
  2.2 4.2 %collective-permute-start.2 = (bf16[1,304,1024]{2,1,0:T(8,128)(2,1)S(1)}, bf16[1,304,1024]{2,1,0:T(8,128)(2,1)S(1)}, u32[]{:S(2)}, u32[]{:S(2)}) collective-permute-start(bf16[1,304,1024]{2,1,0:T(8,128)(2,1)S(1)} %lower.1), channel_id=1, source_target_pairs={{0,6},{1,7},{2,0},{3,1},{4,2},{5,3},{6,4},{7,5},{8,14},{9,15},{10,... | collective-permute-start | bytes 1867784 | tf_op jit(solution)/shard_map/ppermute | solution.py:415
  6.4 1.3 collective-permute-start
  7.7 25.4 %collective-permute-done.2 = bf16[1,304,1024]{2,1,0:T(8,128)(2,1)S(1)} collective-permute-done((bf16[1,304,1024]{2,1,0:T(8,128)(2,1)S(1)}, bf16[1,304,1024]{2,1,0:T(8,128)(2,1)S(1)}, u32[]{:S(2)}, u32[]{:S(2)}) %collective-permute-start.2) | collective-permute-done | bytes 622624 | tf_op jit(solution)/shard_map/ppermute | solution.py:415
  33.1 3.4 %collective-permute-done = bf16[1,304,1024]{2,1,0:T(8,128)(2,1)S(1)} collective-permute-done((bf16[1,304,1024]{2,1,0:T(8,128)(2,1)S(1)}, bf16[1,304,1024]{2,1,0:T(8,128)(2,1)S(1)}, u32[]{:S(2)}, u32[]{:S(2)}) %collective-permute-start) | collective-permute-done | bytes 622624 | tf_op jit(solution)/shard_map/ppermute | solution.py:415
  36.5 0.3 pad_maximum_fusion.same_ref
  36.8 0.1 collective-permute-start.3
  36.9 1.1 cut_up.1
  38.0 20.4 %all_to_all.20.held_ref = bf16[16,160,128]{2,1,0:T(8,128)(2,1)S(1)} all-to-all(bf16[16,160,128]{2,1,0:T(8,128)(2,1)S(1)} %cut_up.1), channel_id=1, replica_groups=mesh['row'=16,'col'=8] {'row'}, dimensions={0} | all-to-all | bytes 1310720 | tf_op jit(solution)/shard_map/all_to_all | solution.py:430
  58.4 2.0 %pick.1 = (bf16[16,3,152,128]{3,2,1,0:T(8,128)(2,1)}, s32[16,128]{1,0:T(8,128)S(1)}) custom-call(bf16[16,160,128]{2,1,0:T(8,128)(2,1)S(1)} %all_to_all.20.held_ref), custom_call_target="tpu_custom_call" | custom-call | tf_op jit(solution)/shard_map/pick/pallas_call | solution.py:109
  60.5 4.6 %all-to-all-start.1 = ((bf16[16,3,152,128]{3,2,1,0:T(8,128)(2,1)}), bf16[16,3,152,128]{3,2,1,0:T(8,128)(2,1)}, u32[]{:S(2)}, u32[]{:S(2)}) async-start(bf16[16,3,152,128]{3,2,1,0:T(8,128)(2,1)} %get-tuple-element.21), calls=%async_computation.1 | async-start | bytes 3735552 | tf_op jit(solution)/shard_map/all_to_all | solution.py:434
  65.1 14.8 %ready.1 = (f32[3,1024,1024]{2,1,0:T(8,128)}, f32[3,1024,1024]{2,1,0:T(8,128)}, bf16[4,304,1024]{2,1,0:T(8,128)(2,1)}, bf16[4,304,1024]{2,1,0:T(8,128)(2,1)}) custom-call(s32[3]{0:T(128)S(1)} %copy-done.8, s32[3]{0:T(128)S(1)} %copy-done.9, s32[3,1024,1024]{2,1,0:T(8,128)} %count_ref.1, f32[128,8,128]{2,1,0:T(8,128)S(1)} %bitcast.16), custom_call_target="tpu_custom_call" | custom-call | tf_op jit(solution)/shard_map/ready/pallas_call | solution.py:186
  79.9 12.9 %all-to-all-done.1.part_ref = bf16[16,3,152,128]{3,2,1,0:T(8,128)(2,1)} async-done(((bf16[16,3,152,128]{3,2,1,0:T(8,128)(2,1)}), bf16[16,3,152,128]{3,2,1,0:T(8,128)(2,1)}, u32[]{:S(2)}, u32[]{:S(2)}) %all-to-all-start.1) | async-done | bytes 1867808 | tf_op jit(solution)/shard_map/all_to_all | solution.py:434
  92.9 15.3 %tile_terms.1 = (bf16[16,3,152,128]{3,2,1,0:T(8,128)(2,1)}, bf16[4,304,1024]{2,1,0:T(8,128)(2,1)}, bf16[4,304,1024]{2,1,0:T(8,128)(2,1)}) custom-call(s32[1]{0:T(128)} %bitcast.2.place, s32[3]{0:T(128)} %rows.3, bf16[16,3,152,128]{3,2,1,0:T(8,128)(2,1)} %all-to-all-done.1.part_ref, ...), custom_call_target="tpu_custom_call", output_to_operand_aliasing={{1}: (7, {}), {2}: (8, {})} | custom-call | tf_op jit(solution)/shard_map/tile_terms/pallas_call | solution.py:288
  108.2 0.1 collective-permute-start.4
  108.3 4.6 %all-to-all-start.2 = ((bf16[16,3,152,128]{3,2,1,0:T(8,128)(2,1)}), bf16[16,3,152,128]{3,2,1,0:T(8,128)(2,1)}, u32[]{:S(2)}, u32[]{:S(2)}) async-start(bf16[16,3,152,128]{3,2,1,0:T(8,128)(2,1)} %get-tuple-element.34), calls=%async_computation.2 | async-start | bytes 3735552 | tf_op jit(solution)/shard_map/all_to_all | solution.py:441
  112.9 0.5 collective-permute-done.4.got_ref
  113.4 3.1 %join.1 = (bf16[304,1024]{1,0:T(8,128)(2,1)S(1)}, bf16[304,1024]{1,0:T(8,128)(2,1)}, bf16[304,1024]{1,0:T(8,128)(2,1)}, bf16[304,1024]{1,0:T(8,128)(2,1)}) custom-call(bf16[4,304,1024]{2,1,0:T(8,128)(2,1)S(1)} %copy-done, bf16[4,304,1024]{2,1,0:T(8,128)(2,1)} %collective-permute-done.4.got_ref), custom_call_target="tpu_custom_call" | custom-call | tf_op jit(solution)/shard_map/join/pallas_call | solution.py:317
  116.5 0.0 collective-permute-start.5
  116.5 2.4 %collective-permute-start.6 = (bf16[304,1024]{1,0:T(8,128)(2,1)}, bf16[304,1024]{1,0:T(8,128)(2,1)}, u32[]{:S(2)}, u32[]{:S(2)}) collective-permute-start(bf16[304,1024]{1,0:T(8,128)(2,1)} %get-tuple-element.30), channel_id=1, source_target_pairs={{0,4},{1,5},{2,6},{3,7},{4,0},{5,1},{6,2},{7,3},{8,12},{9,13},{10,... | collective-permute-start | bytes 1867784 | tf_op jit(solution)/shard_map/ppermute | solution.py:415
  118.8 0.9 collective-permute-start.7
  119.7 24.5 %all-to-all-done.2.term_ref = bf16[16,3,152,128]{3,2,1,0:T(8,128)(2,1)} async-done(((bf16[16,3,152,128]{3,2,1,0:T(8,128)(2,1)}), bf16[16,3,152,128]{3,2,1,0:T(8,128)(2,1)}, u32[]{:S(2)}, u32[]{:S(2)}) %all-to-all-start.2) | async-done | bytes 1867808 | tf_op jit(solution)/shard_map/all_to_all | solution.py:441
  144.2 2.0 %owner_sum.1 = bf16[16,152,128]{2,1,0:T(8,128)(2,1)S(1)} custom-call(s32[16,128]{1,0:T(8,128)S(1)} %get-tuple-element.33.asked, bf16[16,3,152,128]{3,2,1,0:T(8,128)(2,1)} %all-to-all-done.2.term_ref), custom_call_target="tpu_custom_call" | custom-call | tf_op jit(solution)/shard_map/owner_sum/pallas_call | solution.py:335
  146.2 0.0 copy-start.2
  146.2 0.0 copy-start.6
  146.2 15.4 %all_to_all.21.grad_ref = bf16[16,152,128]{2,1,0:T(8,128)(2,1)S(1)} all-to-all(bf16[16,152,128]{2,1,0:T(8,128)(2,1)S(1)} %owner_sum.1), channel_id=1, replica_groups=mesh['row'=16,'col'=8] {'row'}, dimensions={0} | all-to-all | bytes 1245184 | tf_op jit(solution)/shard_map/all_to_all | solution.py:445
  161.7 2.5 %col_update.1 = (f32[2400,128]{1,0:T(8,128)}, f32[2400,128]{1,0:T(8,128)}) custom-call(f32[2400,128]{1,0:T(8,128)S(1)} %bitcast.13, f32[2400,128]{1,0:T(8,128)S(1)} %bitcast.14, bf16[16,152,128]{2,1,0:T(8,128)(2,1)S(1)} %all_to_all.21.grad_ref), custom_call_target="tpu_custom_call" | custom-call | tf_op jit(solution)/shard_map/col_update/pallas_call | solution.py:375
  164.3 4.0 %row_update.1 = (f32[2400,128]{1,0:T(8,128)}, f32[2400,128]{1,0:T(8,128)}) custom-call(f32[2400,128]{1,0:T(8,128)S(1)} %bitcast.11, f32[2400,128]{1,0:T(8,128)S(1)} %bitcast.15, bf16[304,1024]{1,0:T(8,128)(2,1)S(1)} %get-tuple-element.28.refs_0_, bf16[304,1024]{1,0:T(8,128)(2,1)} %collective-permute-done.5.refs_1_, ...), custom_call_target="tpu_custom_call" | custom-call | tf_op jit(solution)/shard_map/row_update/pallas_call | solution.py:404
  (22 shorter events, 0.0 us)
Async XLA Ops:
  0.6 1.3 copy-start.1
  2.2 34.7 %copy-start.3 = (f32[1,300,1024]{2,0,1:T(1,128)S(1)}, f32[1,300,1024]{2,0,1:T(1,128)}, u32[]{:S(2)}) copy-start(f32[1,300,1024]{2,0,1:T(1,128)} %param.9) | copy-start | bytes 3686404
  2.2 34.7 %copy-start.9 = (s32[3]{0:T(128)S(1)}, s32[3]{0:T(128)}, u32[]{:S(2)}) copy-start(s32[3]{0:T(128)} %cols.1) | copy-start | bytes 40
  2.2 30.8 %collective-permute-start.2 = (bf16[1,304,1024]{2,1,0:T(8,128)(2,1)S(1)}, bf16[1,304,1024]{2,1,0:T(8,128)(2,1)S(1)}, u32[]{:S(2)}, u32[]{:S(2)}) collective-permute-start(bf16[1,304,1024]{2,1,0:T(8,128)(2,1)S(1)} %lower.1), channel_id=1, source_target_pairs={{0,6},{1,7},{2,0},{3,1},{4,2},{5,3},{6,4},{7,5},{8,14},{9,15},{10,... | collective-permute-start | bytes 1867784 | tf_op jit(solution)/shard_map/ppermute | solution.py:415
  6.4 26.6 %collective-permute-start.1 = (bf16[1,304,1024]{2,1,0:T(8,128)(2,1)S(1)}, bf16[1,304,1024]{2,1,0:T(8,128)(2,1)S(1)}, u32[]{:S(2)}, u32[]{:S(2)}) collective-permute-start(bf16[1,304,1024]{2,1,0:T(8,128)(2,1)S(1)} %lower.1), channel_id=1, source_target_pairs={{0,4},{1,5},{2,6},{3,7},{4,0},{5,1},{6,2},{7,3},{8,12},{9,13},{10,... | collective-permute-start | bytes 1867784 | tf_op jit(solution)/shard_map/ppermute | solution.py:415
  6.4 30.0 %collective-permute-start = (bf16[1,304,1024]{2,1,0:T(8,128)(2,1)S(1)}, bf16[1,304,1024]{2,1,0:T(8,128)(2,1)S(1)}, u32[]{:S(2)}, u32[]{:S(2)}) collective-permute-start(bf16[1,304,1024]{2,1,0:T(8,128)(2,1)S(1)} %lower.1), channel_id=1, source_target_pairs={{0,2},{1,3},{2,4},{3,5},{4,6},{5,7},{6,0},{7,1},{8,10},{9,11},{10,... | collective-permute-start | bytes 1867784 | tf_op jit(solution)/shard_map/ppermute | solution.py:415
  36.8 23.7 %copy-start.10 = (bf16[4,304,1024]{2,1,0:T(8,128)(2,1)}, bf16[4,304,1024]{2,1,0:T(8,128)(2,1)S(1)}, u32[]{:S(2)}) copy-start(bf16[4,304,1024]{2,1,0:T(8,128)(2,1)S(1)} %pad_maximum_fusion.same_ref) | copy-start | bytes 7471108
  36.8 56.1 %collective-permute-start.3 = (bf16[4,304,1024]{2,1,0:T(8,128)(2,1)S(1)}, bf16[4,304,1024]{2,1,0:T(8,128)(2,1)}, u32[]{:S(2)}, u32[]{:S(2)}) collective-permute-start(bf16[4,304,1024]{2,1,0:T(8,128)(2,1)S(1)} %pad_maximum_fusion.same_ref), channel_id=1, source_target_pairs={{0,1},{1,0},{2,3},{3,2},{4,5},{5,4},{6,7},{7,6},{8,9},{9,8},{10,11... | collective-permute-start | bytes 7471112 | tf_op jit(solution)/shard_map/ppermute | solution.py:419
  58.4 6.7 %copy-start.7 = (f32[131072]{0:T(1024)S(1)}, f32[131072]{0:T(1024)}, u32[]{:S(2)}) copy-start(f32[131072]{0:T(1024)} %param.12) | copy-start | bytes 1572868
  58.4 6.7 %copy-start.8 = (s32[3]{0:T(128)S(1)}, s32[3]{0:T(128)}, u32[]{:S(2)}) copy-start(s32[3]{0:T(128)} %rows.3) | copy-start | bytes 40
  60.5 32.4 %all-to-all-start.1 = ((bf16[16,3,152,128]{3,2,1,0:T(8,128)(2,1)}), bf16[16,3,152,128]{3,2,1,0:T(8,128)(2,1)}, u32[]{:S(2)}, u32[]{:S(2)}) async-start(bf16[16,3,152,128]{3,2,1,0:T(8,128)(2,1)} %get-tuple-element.21), calls=%async_computation.1 | async-start | bytes 3735552 | tf_op jit(solution)/shard_map/all_to_all | solution.py:434
  108.2 5.2 %copy-start = (bf16[4,304,1024]{2,1,0:T(8,128)(2,1)S(1)}, bf16[4,304,1024]{2,1,0:T(8,128)(2,1)}, u32[]{:S(2)}) copy-start(bf16[4,304,1024]{2,1,0:T(8,128)(2,1)} %get-tuple-element.26.keep_ref) | copy-start | bytes 7471108
  108.2 5.1 %collective-permute-start.4 = (bf16[4,304,1024]{2,1,0:T(8,128)(2,1)}, bf16[4,304,1024]{2,1,0:T(8,128)(2,1)}, u32[]{:S(2)}, u32[]{:S(2)}) collective-permute-start(bf16[4,304,1024]{2,1,0:T(8,128)(2,1)} %get-tuple-element.27), channel_id=1, source_target_pairs={{0,1},{1,0},{2,3},{3,2},{4,5},{5,4},{6,7},{7,6},{8,9},{9,8},{10,11... | collective-permute-start | bytes 7471112 | tf_op jit(solution)/shard_map/ppermute | solution.py:419
  108.3 35.9 %all-to-all-start.2 = ((bf16[16,3,152,128]{3,2,1,0:T(8,128)(2,1)}), bf16[16,3,152,128]{3,2,1,0:T(8,128)(2,1)}, u32[]{:S(2)}, u32[]{:S(2)}) async-start(bf16[16,3,152,128]{3,2,1,0:T(8,128)(2,1)} %get-tuple-element.34), calls=%async_computation.2 | async-start | bytes 3735552 | tf_op jit(solution)/shard_map/all_to_all | solution.py:441
  116.5 45.2 %copy-start.4 = (f32[1,300,1024]{2,0,1:T(1,128)S(1)}, f32[1,300,1024]{2,0,1:T(1,128)}, u32[]{:S(2)}) copy-start(f32[1,300,1024]{2,0,1:T(1,128)} %param.9) | copy-start | bytes 3686404
  116.5 45.2 %copy-start.5 = (f32[1,300,1024]{2,0,1:T(1,128)S(1)}, f32[1,300,1024]{2,0,1:T(1,128)}, u32[]{:S(2)}) copy-start(f32[1,300,1024]{2,0,1:T(1,128)} %param.11) | copy-start | bytes 3686404
  116.5 47.8 %collective-permute-start.5 = (bf16[304,1024]{1,0:T(8,128)(2,1)}, bf16[304,1024]{1,0:T(8,128)(2,1)}, u32[]{:S(2)}, u32[]{:S(2)}) collective-permute-start(bf16[304,1024]{1,0:T(8,128)(2,1)} %get-tuple-element.29), channel_id=1, source_target_pairs={{0,2},{1,3},{2,4},{3,5},{4,6},{5,7},{6,0},{7,1},{8,10},{9,11},{10,... | collective-permute-start | bytes 1867784 | tf_op jit(solution)/shard_map/ppermute | solution.py:415
  116.5 47.8 %collective-permute-start.6 = (bf16[304,1024]{1,0:T(8,128)(2,1)}, bf16[304,1024]{1,0:T(8,128)(2,1)}, u32[]{:S(2)}, u32[]{:S(2)}) collective-permute-start(bf16[304,1024]{1,0:T(8,128)(2,1)} %get-tuple-element.30), channel_id=1, source_target_pairs={{0,4},{1,5},{2,6},{3,7},{4,0},{5,1},{6,2},{7,3},{8,12},{9,13},{10,... | collective-permute-start | bytes 1867784 | tf_op jit(solution)/shard_map/ppermute | solution.py:415
  118.8 45.4 %collective-permute-start.7 = (bf16[304,1024]{1,0:T(8,128)(2,1)}, bf16[304,1024]{1,0:T(8,128)(2,1)}, u32[]{:S(2)}, u32[]{:S(2)}) collective-permute-start(bf16[304,1024]{1,0:T(8,128)(2,1)} %get-tuple-element.31), channel_id=1, source_target_pairs={{0,6},{1,7},{2,0},{3,1},{4,2},{5,3},{6,4},{7,5},{8,14},{9,15},{10,... | collective-permute-start | bytes 1867784 | tf_op jit(solution)/shard_map/ppermute | solution.py:415
  146.2 18.1 %copy-start.2 = (f32[1,300,1024]{2,0,1:T(1,128)S(1)}, f32[1,300,1024]{2,0,1:T(1,128)}, u32[]{:S(2)}) copy-start(f32[1,300,1024]{2,0,1:T(1,128)} %param.8) | copy-start | bytes 3686404
  146.2 18.1 %copy-start.6 = (f32[1,300,1024]{2,0,1:T(1,128)S(1)}, f32[1,300,1024]{2,0,1:T(1,128)}, u32[]{:S(2)}) copy-start(f32[1,300,1024]{2,0,1:T(1,128)} %param.10) | copy-start | bytes 3686404

commit v3 on v2

--- a/solution.py
+++ b/solution.py
@@ -27,6 +27,10 @@
 SMEM = pl.BlockSpec(memory_space=pltpu.SMEM)
 VMEM = pl.BlockSpec(memory_space=pltpu.VMEM)
 HBM = pl.BlockSpec(memory_space=pl.ANY)
+
+
+def in_hbm(array):
+    return pltpu.with_memory_space_constraint(array, pltpu.HBM)
 
 
 def span(first, length, n):
@@ -66,7 +70,7 @@
         scratch_shapes=[pltpu.VMEM((DIM * GROUPS, LANES), f32), pltpu.SemaphoreType.DMA((2,))],
         compiler_params=pltpu.CompilerParams(vmem_limit_bytes=8 << 20),
         name="cut_up",
-    )(tile_cols, col_emb)
+    )(in_hbm(tile_cols), in_hbm(col_emb))
 
 
 def low_kernel(row_ref, low_ref):
@@ -305,7 +309,7 @@
         input_output_aliases={7: 1, 8: 2},
         compiler_params=pltpu.CompilerParams(vmem_limit_bytes=60 << 20),
         name="tile_terms",
-    )(place, tile_rows, parts, same, other, weight, offset, blank, other_blank)
+    )(place, tile_rows, in_hbm(parts), in_hbm(same), in_hbm(other), weight, offset, blank, other_blank)
 
 
 def join_kernel(keep_ref, got_ref, *out_refs):
@@ -323,24 +327,44 @@
     )(keep, got)
 
 
-def owner_sum_kernel(asked, term_ref, out_ref, total):
+def owner_sum_kernel(asked, term_ref, out_ref, terms, total, sums, sems):
+    quarter = PARTS // 4
+    moves = []
+    for q in range(4):
+        some = pl.ds(q * quarter, quarter)
+        moves.append(pltpu.make_async_copy(term_ref.at[some], terms.at[some], sems.at[q]))
+        moves[q].start()
     total[...] = jnp.zeros((PARTS, HALF, LANES), f32)
-    for d in range(PARTS):
-        for t in range(TILES):
-            total[asked[d, t]] += term_ref[d, t].astype(f32)
-    out_ref[...] = total[...].astype(bf16)
+    for q in range(4):
+        moves[q].wait()
+        for d in range(q * quarter, (q + 1) * quarter):
+            for t in range(TILES):
+                total[asked[d, t]] += terms[d, t].astype(f32)
+    outs = []
+    for q in range(4):
+        some = pl.ds(q * quarter, quarter)
+        sums[some] = total[some].astype(bf16)
+        outs.append(pltpu.make_async_copy(sums.at[some], out_ref.at[some], sems.at[4 + q]))
+        outs[q].start()
+    for out in outs:
+        out.wait()
 
 
 def owner_sum(asked, terms):
     return pl.pallas_call(
         owner_sum_kernel,
-        out_shape=jax.ShapeDtypeStruct((PARTS, HALF, LANES), bf16),
-        in_specs=[SMEM, VMEM],
-        out_specs=VMEM,
-        scratch_shapes=[pltpu.VMEM((PARTS, HALF, LANES), f32)],
+        out_shape=pltpu.HBM((PARTS, HALF, LANES), bf16),
+        in_specs=[SMEM, HBM],
+        out_specs=HBM,
+        scratch_shapes=[
+            pltpu.VMEM((PARTS, TILES, HALF, LANES), bf16),
+            pltpu.VMEM((PARTS, HALF, LANES), f32),
+            pltpu.VMEM((PARTS, HALF, LANES), bf16),
+            pltpu.SemaphoreType.DMA((8,)),
+        ],
         compiler_params=pltpu.CompilerParams(vmem_limit_bytes=12 << 20),
         name="owner_sum",
-    )(asked, terms)
+    )(asked, in_hbm(terms))
 
 
 def adagrad(weights, history, gradient):
@@ -385,7 +409,7 @@
         ],
         compiler_params=pltpu.CompilerParams(vmem_limit_bytes=12 << 20),
         name="col_update",
-    )(emb, acc, grad)
+    )(in_hbm(emb), in_hbm(acc), grad)
     return new_emb.reshape(1, DIM, BLOCK), new_acc.reshape(1, DIM, BLOCK)
 
 

time: 169 us -> 171 us (1.012)
  transfers between devices with their start and end apart: 10 -> 10, of which waited for: 5 -> 5; matrix products, arithmetic and copies ran while one was open for 0% -> 0% of each run, Pallas kernels for 15% -> 17%
where the time goes in v3:
time: 171 us; the launch traced here: 170 us
  waiting for transfers between devices  66.6 us (39%)
  Pallas kernels  46.4 us (27%)
  blocking collectives  36.6 us (21%)
  starting transfers between devices  18.1 us (11%)
    ppermute x6, waiting for transfers between devices, send_along_z(): lax.ppermute(array, 'col', [(i, (i + 2 * step) % COLS) for i in range(COL...  28.8 us
    all_to_all x1, waiting for transfers between devices, body(): terms = lax.all_to_all(terms, 'row', 0, 0, tiled=True)  24.5 us
    all_to_all x1, blocking collectives, body(): held = lax.all_to_all(slices, 'row', 0, 0, tiled=True)  20.4 us
    all_to_all x1, blocking collectives, body(): col_sum = lax.all_to_all(sums, 'row', 0, 0, tiled=True)  16.2 us
    pallas_call x1, Pallas kernels, tile_terms(): pl.pallas_call(tile_kernel, in_specs=[SMEM, SMEM] + [HBM] * 7, out_specs=...  15.3 us
    pallas_call x1, Pallas kernels, ready(): pl.pallas_call(ready_kernel, grid_spec=grid_spec, out_shape=(jax.ShapeDty...  14.8 us
    all_to_all x1, waiting for transfers between devices, body(): parts = lax.all_to_all(picked, 'row', 0, 0, tiled=True)  12.8 us
    ppermute x6, starting transfers between devices, send_along_z(): lax.ppermute(array, 'col', [(i, (i + 2 * step) % COLS) for i in range(COL...  8.72 us
  transfers between devices with their start and end apart: 10, of which 5 were waited for; matrix products, arithmetic and copies ran while one was open for 0% of the time, Pallas kernels for 17%

profile of v3, /device:TPU:0, one launch (start us, length us, event | category | flops | bytes accessed | tf_op | source)
XLA Modules:
  0.0 170.1 jit_solution(13595695773626718224)
XLA Ops:
  0.6 0.0 copy-start.1
  0.6 1.3 copy-done.1
  1.9 0.3 lower.1
  2.2 4.2 %collective-permute-start.2 = (bf16[1,304,1024]{2,1,0:T(8,128)(2,1)S(1)}, bf16[1,304,1024]{2,1,0:T(8,128)(2,1)S(1)}, u32[]{:S(2)}, u32[]{:S(2)}) collective-permute-start(bf16[1,304,1024]{2,1,0:T(8,128)(2,1)S(1)} %lower.1), channel_id=1, source_target_pairs={{0,6},{1,7},{2,0},{3,1},{4,2},{5,3},{6,4},{7,5},{8,14},{9,15},{10,... | collective-permute-start | bytes 1867784 | tf_op jit(solution)/shard_map/ppermute | solution.py:439
  6.4 0.0 collective-permute-start.1
  6.4 1.3 collective-permute-start
  7.7 25.4 %collective-permute-done.2 = bf16[1,304,1024]{2,1,0:T(8,128)(2,1)S(1)} collective-permute-done((bf16[1,304,1024]{2,1,0:T(8,128)(2,1)S(1)}, bf16[1,304,1024]{2,1,0:T(8,128)(2,1)S(1)}, u32[]{:S(2)}, u32[]{:S(2)}) %collective-permute-start.2) | collective-permute-done | bytes 622624 | tf_op jit(solution)/shard_map/ppermute | solution.py:439
  33.0 3.4 %collective-permute-done = bf16[1,304,1024]{2,1,0:T(8,128)(2,1)S(1)} collective-permute-done((bf16[1,304,1024]{2,1,0:T(8,128)(2,1)S(1)}, bf16[1,304,1024]{2,1,0:T(8,128)(2,1)S(1)}, u32[]{:S(2)}, u32[]{:S(2)}) %collective-permute-start) | collective-permute-done | bytes 622624 | tf_op jit(solution)/shard_map/ppermute | solution.py:439
  36.5 0.3 pad_maximum_fusion.same_ref
  36.8 0.1 collective-permute-start.3
  36.9 2.1 %cut_up.1 = bf16[16,160,128]{2,1,0:T(8,128)(2,1)S(1)} custom-call(s32[3]{0:T(128)} %cols.1, f32[2400,128]{1,0:T(8,128)} %bitcast.14), custom_call_target="tpu_custom_call" | custom-call | tf_op jit(solution)/shard_map/cut_up/pallas_call | solution.py:65
  39.0 20.4 %all_to_all.20.held_ref = bf16[16,160,128]{2,1,0:T(8,128)(2,1)S(1)} all-to-all(bf16[16,160,128]{2,1,0:T(8,128)(2,1)S(1)} %cut_up.1), channel_id=1, replica_groups=mesh['row'=16,'col'=8] {'row'}, dimensions={0} | all-to-all | bytes 1310720 | tf_op jit(solution)/shard_map/all_to_all | solution.py:454
  59.4 2.0 %pick.1 = (bf16[16,3,152,128]{3,2,1,0:T(8,128)(2,1)}, s32[16,128]{1,0:T(8,128)S(1)}) custom-call(bf16[16,160,128]{2,1,0:T(8,128)(2,1)S(1)} %all_to_all.20.held_ref), custom_call_target="tpu_custom_call" | custom-call | tf_op jit(solution)/shard_map/pick/pallas_call | solution.py:113
  61.4 4.6 %all-to-all-start.1 = ((bf16[16,3,152,128]{3,2,1,0:T(8,128)(2,1)}), bf16[16,3,152,128]{3,2,1,0:T(8,128)(2,1)}, u32[]{:S(2)}, u32[]{:S(2)}) async-start(bf16[16,3,152,128]{3,2,1,0:T(8,128)(2,1)} %get-tuple-element.21), calls=%async_computation.1 | async-start | bytes 3735552 | tf_op jit(solution)/shard_map/all_to_all | solution.py:458
  66.1 14.8 %ready.1 = (f32[3,1024,1024]{2,1,0:T(8,128)}, f32[3,1024,1024]{2,1,0:T(8,128)}, bf16[4,304,1024]{2,1,0:T(8,128)(2,1)}, bf16[4,304,1024]{2,1,0:T(8,128)(2,1)}) custom-call(s32[3]{0:T(128)S(1)} %copy-done.5, s32[3]{0:T(128)S(1)} %copy-done.6, s32[3,1024,1024]{2,1,0:T(8,128)} %count_ref.1, f32[128,8,128]{2,1,0:T(8,128)S(1)} %bitcast.13), custom_call_target="tpu_custom_call" | custom-call | tf_op jit(solution)/shard_map/ready/pallas_call | solution.py:190
  80.9 12.8 %all-to-all-done.1.part_ref = bf16[16,3,152,128]{3,2,1,0:T(8,128)(2,1)} async-done(((bf16[16,3,152,128]{3,2,1,0:T(8,128)(2,1)}), bf16[16,3,152,128]{3,2,1,0:T(8,128)(2,1)}, u32[]{:S(2)}, u32[]{:S(2)}) %all-to-all-start.1) | async-done | bytes 1867808 | tf_op jit(solution)/shard_map/all_to_all | solution.py:458
  93.7 0.0 collective-permute-done.3.other_ref
  93.7 15.3 %tile_terms.1 = (bf16[16,3,152,128]{3,2,1,0:T(8,128)(2,1)}, bf16[4,304,1024]{2,1,0:T(8,128)(2,1)}, bf16[4,304,1024]{2,1,0:T(8,128)(2,1)}) custom-call(s32[1]{0:T(128)} %bitcast.2.place, s32[3]{0:T(128)} %rows.3, bf16[16,3,152,128]{3,2,1,0:T(8,128)(2,1)} %all-to-all-done.1.part_ref, ...), custom_call_target="tpu_custom_call", output_to_operand_aliasing={{1}: (7, {}), {2}: (8, {})} | custom-call | tf_op jit(solution)/shard_map/tile_terms/pallas_call | solution.py:292
  109.0 0.1 collective-permute-start.4
  109.1 4.6 %all-to-all-start.2 = ((bf16[16,3,152,128]{3,2,1,0:T(8,128)(2,1)}), bf16[16,3,152,128]{3,2,1,0:T(8,128)(2,1)}, u32[]{:S(2)}, u32[]{:S(2)}) async-start(bf16[16,3,152,128]{3,2,1,0:T(8,128)(2,1)} %get-tuple-element.34), calls=%async_computation.2 | async-start | bytes 3735552 | tf_op jit(solution)/shard_map/all_to_all | solution.py:465
  113.6 0.5 collective-permute-done.4.got_ref
  114.1 3.1 %join.1 = (bf16[304,1024]{1,0:T(8,128)(2,1)S(1)}, bf16[304,1024]{1,0:T(8,128)(2,1)}, bf16[304,1024]{1,0:T(8,128)(2,1)}, bf16[304,1024]{1,0:T(8,128)(2,1)}) custom-call(bf16[4,304,1024]{2,1,0:T(8,128)(2,1)S(1)} %copy-done, bf16[4,304,1024]{2,1,0:T(8,128)(2,1)} %collective-permute-done.4.got_ref), custom_call_target="tpu_custom_call" | custom-call | tf_op jit(solution)/shard_map/join/pallas_call | solution.py:321
  117.2 2.3 %collective-permute-start.6 = (bf16[304,1024]{1,0:T(8,128)(2,1)}, bf16[304,1024]{1,0:T(8,128)(2,1)S(1)}, u32[]{:S(2)}, u32[]{:S(2)}) collective-permute-start(bf16[304,1024]{1,0:T(8,128)(2,1)} %get-tuple-element.30), channel_id=1, source_target_pairs={{0,4},{1,5},{2,6},{3,7},{4,0},{5,1},{6,2},{7,3},{8,12},{9,13},{10,... | collective-permute-start | bytes 1867784 | tf_op jit(solution)/shard_map/ppermute | solution.py:439
  119.6 0.9 collective-permute-start.7
  120.5 24.5 %all-to-all-done.2.term_ref = bf16[16,3,152,128]{3,2,1,0:T(8,128)(2,1)} async-done(((bf16[16,3,152,128]{3,2,1,0:T(8,128)(2,1)}), bf16[16,3,152,128]{3,2,1,0:T(8,128)(2,1)}, u32[]{:S(2)}, u32[]{:S(2)}) %all-to-all-start.2) | async-done | bytes 1867808 | tf_op jit(solution)/shard_map/all_to_all | solution.py:465
  145.0 3.1 %owner_sum.1 = bf16[16,152,128]{2,1,0:T(8,128)(2,1)} custom-call(s32[16,128]{1,0:T(8,128)S(1)} %get-tuple-element.33.asked, bf16[16,3,152,128]{3,2,1,0:T(8,128)(2,1)} %all-to-all-done.2.term_ref), custom_call_target="tpu_custom_call" | custom-call | tf_op jit(solution)/shard_map/owner_sum/pallas_call | solution.py:354
  148.1 0.0 copy-start.2
  148.1 0.0 copy-start.3
  148.1 16.2 %all_to_all.21.grad_ref = bf16[16,152,128]{2,1,0:T(8,128)(2,1)S(1)} all-to-all(bf16[16,152,128]{2,1,0:T(8,128)(2,1)} %owner_sum.1), channel_id=1, replica_groups=mesh['row'=16,'col'=8] {'row'}, dimensions={0} | all-to-all | bytes 1245184 | tf_op jit(solution)/shard_map/all_to_all | solution.py:469
  164.3 3.2 %col_update.1 = (f32[2400,128]{1,0:T(8,128)}, f32[2400,128]{1,0:T(8,128)}) custom-call(f32[2400,128]{1,0:T(8,128)} %bitcast.15, f32[2400,128]{1,0:T(8,128)} %bitcast.16, bf16[16,152,128]{2,1,0:T(8,128)(2,1)S(1)} %all_to_all.21.grad_ref), custom_call_target="tpu_custom_call" | custom-call | tf_op jit(solution)/shard_map/col_update/pallas_call | solution.py:399
  167.5 0.0 collective-permute-done.7.refs_3_
  167.6 2.6 %row_update.1 = (f32[2400,128]{1,0:T(8,128)}, f32[2400,128]{1,0:T(8,128)}) custom-call(f32[2400,128]{1,0:T(8,128)S(1)} %bitcast.11, f32[2400,128]{1,0:T(8,128)S(1)} %bitcast.12, bf16[304,1024]{1,0:T(8,128)(2,1)S(1)} %get-tuple-element.28.refs_0_, bf16[304,1024]{1,0:T(8,128)(2,1)S(1)} %collective-permute-done.5.refs_1_, ...), custom_call_target="tpu_custom_call" | custom-call | tf_op jit(solution)/shard_map/row_update/pallas_call | solution.py:428
  (16 shorter events, 0.0 us)
Async XLA Ops:
  0.6 1.3 copy-start.1
  2.2 30.8 %collective-permute-start.2 = (bf16[1,304,1024]{2,1,0:T(8,128)(2,1)S(1)}, bf16[1,304,1024]{2,1,0:T(8,128)(2,1)S(1)}, u32[]{:S(2)}, u32[]{:S(2)}) collective-permute-start(bf16[1,304,1024]{2,1,0:T(8,128)(2,1)S(1)} %lower.1), channel_id=1, source_target_pairs={{0,6},{1,7},{2,0},{3,1},{4,2},{5,3},{6,4},{7,5},{8,14},{9,15},{10,... | collective-permute-start | bytes 1867784 | tf_op jit(solution)/shard_map/ppermute | solution.py:439
  6.4 26.6 %collective-permute-start.1 = (bf16[1,304,1024]{2,1,0:T(8,128)(2,1)S(1)}, bf16[1,304,1024]{2,1,0:T(8,128)(2,1)S(1)}, u32[]{:S(2)}, u32[]{:S(2)}) collective-permute-start(bf16[1,304,1024]{2,1,0:T(8,128)(2,1)S(1)} %lower.1), channel_id=1, source_target_pairs={{0,4},{1,5},{2,6},{3,7},{4,0},{5,1},{6,2},{7,3},{8,12},{9,13},{10,... | collective-permute-start | bytes 1867784 | tf_op jit(solution)/shard_map/ppermute | solution.py:439
  6.4 30.0 %collective-permute-start = (bf16[1,304,1024]{2,1,0:T(8,128)(2,1)S(1)}, bf16[1,304,1024]{2,1,0:T(8,128)(2,1)S(1)}, u32[]{:S(2)}, u32[]{:S(2)}) collective-permute-start(bf16[1,304,1024]{2,1,0:T(8,128)(2,1)S(1)} %lower.1), channel_id=1, source_target_pairs={{0,2},{1,3},{2,4},{3,5},{4,6},{5,7},{6,0},{7,1},{8,10},{9,11},{10,... | collective-permute-start | bytes 1867784 | tf_op jit(solution)/shard_map/ppermute | solution.py:439
  36.8 24.6 %copy-start.7 = (bf16[4,304,1024]{2,1,0:T(8,128)(2,1)}, bf16[4,304,1024]{2,1,0:T(8,128)(2,1)S(1)}, u32[]{:S(2)}) copy-start(bf16[4,304,1024]{2,1,0:T(8,128)(2,1)S(1)} %pad_maximum_fusion.same_ref) | copy-start | bytes 7471108
  36.8 56.9 %collective-permute-start.3 = (bf16[4,304,1024]{2,1,0:T(8,128)(2,1)S(1)}, bf16[4,304,1024]{2,1,0:T(8,128)(2,1)}, u32[]{:S(2)}, u32[]{:S(2)}) collective-permute-start(bf16[4,304,1024]{2,1,0:T(8,128)(2,1)S(1)} %pad_maximum_fusion.same_ref), channel_id=1, source_target_pairs={{0,1},{1,0},{2,3},{3,2},{4,5},{5,4},{6,7},{7,6},{8,9},{9,8},{10,11... | collective-permute-start | bytes 7471112 | tf_op jit(solution)/shard_map/ppermute | solution.py:443
  59.4 6.7 %copy-start.4 = (f32[131072]{0:T(1024)S(1)}, f32[131072]{0:T(1024)}, u32[]{:S(2)}) copy-start(f32[131072]{0:T(1024)} %param.12) | copy-start | bytes 1572868
  59.4 6.7 %copy-start.5 = (s32[3]{0:T(128)S(1)}, s32[3]{0:T(128)}, u32[]{:S(2)}) copy-start(s32[3]{0:T(128)} %rows.3) | copy-start | bytes 40
  59.4 6.7 %copy-start.6 = (s32[3]{0:T(128)S(1)}, s32[3]{0:T(128)}, u32[]{:S(2)}) copy-start(s32[3]{0:T(128)} %cols.1) | copy-start | bytes 40
  61.4 32.3 %all-to-all-start.1 = ((bf16[16,3,152,128]{3,2,1,0:T(8,128)(2,1)}), bf16[16,3,152,128]{3,2,1,0:T(8,128)(2,1)}, u32[]{:S(2)}, u32[]{:S(2)}) async-start(bf16[16,3,152,128]{3,2,1,0:T(8,128)(2,1)} %get-tuple-element.21), calls=%async_computation.1 | async-start | bytes 3735552 | tf_op jit(solution)/shard_map/all_to_all | solution.py:458
  109.0 5.2 %copy-start = (bf16[4,304,1024]{2,1,0:T(8,128)(2,1)S(1)}, bf16[4,304,1024]{2,1,0:T(8,128)(2,1)}, u32[]{:S(2)}) copy-start(bf16[4,304,1024]{2,1,0:T(8,128)(2,1)} %get-tuple-element.26.keep_ref) | copy-start | bytes 7471108
  109.0 5.1 %collective-permute-start.4 = (bf16[4,304,1024]{2,1,0:T(8,128)(2,1)}, bf16[4,304,1024]{2,1,0:T(8,128)(2,1)}, u32[]{:S(2)}, u32[]{:S(2)}) collective-permute-start(bf16[4,304,1024]{2,1,0:T(8,128)(2,1)} %get-tuple-element.27), channel_id=1, source_target_pairs={{0,1},{1,0},{2,3},{3,2},{4,5},{5,4},{6,7},{7,6},{8,9},{9,8},{10,11... | collective-permute-start | bytes 7471112 | tf_op jit(solution)/shard_map/ppermute | solution.py:443
  109.1 35.9 %all-to-all-start.2 = ((bf16[16,3,152,128]{3,2,1,0:T(8,128)(2,1)}), bf16[16,3,152,128]{3,2,1,0:T(8,128)(2,1)}, u32[]{:S(2)}, u32[]{:S(2)}) async-start(bf16[16,3,152,128]{3,2,1,0:T(8,128)(2,1)} %get-tuple-element.34), calls=%async_computation.2 | async-start | bytes 3735552 | tf_op jit(solution)/shard_map/all_to_all | solution.py:465
  117.2 50.3 %collective-permute-start.5 = (bf16[304,1024]{1,0:T(8,128)(2,1)}, bf16[304,1024]{1,0:T(8,128)(2,1)S(1)}, u32[]{:S(2)}, u32[]{:S(2)}) collective-permute-start(bf16[304,1024]{1,0:T(8,128)(2,1)} %get-tuple-element.29), channel_id=1, source_target_pairs={{0,2},{1,3},{2,4},{3,5},{4,6},{5,7},{6,0},{7,1},{8,10},{9,11},{10,... | collective-permute-start | bytes 1867784 | tf_op jit(solution)/shard_map/ppermute | solution.py:439
  117.2 50.3 %collective-permute-start.6 = (bf16[304,1024]{1,0:T(8,128)(2,1)}, bf16[304,1024]{1,0:T(8,128)(2,1)S(1)}, u32[]{:S(2)}, u32[]{:S(2)}) collective-permute-start(bf16[304,1024]{1,0:T(8,128)(2,1)} %get-tuple-element.30), channel_id=1, source_target_pairs={{0,4},{1,5},{2,6},{3,7},{4,0},{5,1},{6,2},{7,3},{8,12},{9,13},{10,... | collective-permute-start | bytes 1867784 | tf_op jit(solution)/shard_map/ppermute | solution.py:439
  119.6 47.9 %collective-permute-start.7 = (bf16[304,1024]{1,0:T(8,128)(2,1)}, bf16[304,1024]{1,0:T(8,128)(2,1)S(1)}, u32[]{:S(2)}, u32[]{:S(2)}) collective-permute-start(bf16[304,1024]{1,0:T(8,128)(2,1)} %get-tuple-element.31), channel_id=1, source_target_pairs={{0,6},{1,7},{2,0},{3,1},{4,2},{5,3},{6,4},{7,5},{8,14},{9,15},{10,... | collective-permute-start | bytes 1867784 | tf_op jit(solution)/shard_map/ppermute | solution.py:439
  148.1 19.5 %copy-start.2 = (f32[1,300,1024]{2,0,1:T(1,128)S(1)}, f32[1,300,1024]{2,0,1:T(1,128)}, u32[]{:S(2)}) copy-start(f32[1,300,1024]{2,0,1:T(1,128)} %param.8) | copy-start | bytes 3686404
  148.1 19.5 %copy-start.3 = (f32[1,300,1024]{2,0,1:T(1,128)S(1)}, f32[1,300,1024]{2,0,1:T(1,128)}, u32[]{:S(2)}) copy-start(f32[1,300,1024]{2,0,1:T(1,128)} %param.10) | copy-start | bytes 3686404

commit v4 on v3

--- a/solution.py
+++ b/solution.py
@@ -1,3 +1,5 @@
+import functools
+
 import jax
 import jax.numpy as jnp
 from jax import lax
@@ -20,6 +22,7 @@
 COLS = 8
 FIRST = 512
 GROUPS = 8
+ROW_CUT = 160
 
 f32 = jnp.float32
 bf16 = jnp.bfloat16
@@ -29,6 +32,10 @@
 HBM = pl.BlockSpec(memory_space=pl.ANY)
 
 
+def in_vmem(array):
+    return pltpu.with_memory_space_constraint(array, pltpu.VMEM)
+
+
 def in_hbm(array):
     return pltpu.with_memory_space_constraint(array, pltpu.HBM)
 
@@ -37,7 +44,7 @@
     return pl.ds(first * GROUPS + n, length, stride=GROUPS)
 
 
-def cut_kernel(wanted, col_ref, slice_ref, col, sems):
+def cut_kernel(wanted, col_ref, slice_ref, col, cut, sems):
     edge = HALF * GROUPS
     moves = [
         pltpu.make_async_copy(col_ref.at[:edge], col.at[:edge], sems.at[0]),
@@ -52,25 +59,34 @@
     moves[0].wait()
     for n in range(GROUPS):
         top = jnp.concatenate([col[span(0, HALF, n), :], meta], axis=0)
-        slice_ref[2 * n] = top.astype(bf16)
+        cut[0, n] = top.astype(bf16)
+    outs = [pltpu.make_async_copy(cut.at[h], slice_ref.at[:, h], sems.at[2 + h]) for h in range(2)]
+    outs[0].start()
     moves[1].wait()
     for n in range(GROUPS):
         last = pltpu.roll(col[span(DIM - 8, 8, n), :], 4, 0)
         last = jnp.where(spot < 4, last, 0.0)
         low = jnp.concatenate([col[span(HALF, DIM - 4 - HALF, n), :], last, meta], axis=0)
-        slice_ref[2 * n + 1] = low.astype(bf16)
+        cut[1, n] = low.astype(bf16)
+    outs[1].start()
+    for out in outs:
+        out.wait()
 
 
 def cut_up(tile_cols, col_emb):
     return pl.pallas_call(
         cut_kernel,
-        out_shape=jax.ShapeDtypeStruct((PARTS, META, LANES), bf16),
+        out_shape=pltpu.HBM((GROUPS, 2, META, LANES), bf16),
         in_specs=[SMEM, HBM],
-        out_specs=VMEM,
-        scratch_shapes=[pltpu.VMEM((DIM * GROUPS, LANES), f32), pltpu.SemaphoreType.DMA((2,))],
+        out_specs=HBM,
+        scratch_shapes=[
+            pltpu.VMEM((DIM * GROUPS, LANES), f32),
+            pltpu.VMEM((2, GROUPS, META, LANES), bf16),
+            pltpu.SemaphoreType.DMA((4,)),
+        ],
         compiler_params=pltpu.CompilerParams(vmem_limit_bytes=8 << 20),
         name="cut_up",
-    )(in_hbm(tile_cols), in_hbm(col_emb))
+    )(in_hbm(tile_cols), in_hbm(col_emb)).reshape(PARTS, META, LANES)
 
 
 def low_kernel(row_ref, low_ref):
@@ -129,30 +145,29 @@
     )(held)
 
 
-def ready_kernel(
-    rows, cols, count_ref, margin_ref, weight_ref, offset_ref, blank_ref, other_blank_ref,
-    margin, zero, sems,
-):
+def ready_kernel(base, count, rows, cols, count_ref, margin_ref, weight_ref, offset_ref, *refs):
+    blank_refs, (margin, zero, sems) = refs[:-3], refs[-3:]
     t = pl.program_id(0)
 
     def margin_moves(k):
         return [
-            pltpu.make_async_copy(margin_ref.at[rows[k]], margin.at[k, 0], sems.at[2 * k]),
-            pltpu.make_async_copy(margin_ref.at[cols[k]], margin.at[k, 1], sems.at[2 * k + 1]),
+            pltpu.make_async_copy(margin_ref.at[rows[base + k]], margin.at[k, 0], sems.at[2 * k]),
+            pltpu.make_async_copy(margin_ref.at[cols[base + k]], margin.at[k, 1], sems.at[2 * k + 1]),
         ]
 
     blank_moves = [
         pltpu.make_async_copy(zero, ref.at[s], sems.at[2 * TILES + 4 * i + s])
-        for i, ref in enumerate((blank_ref, other_blank_ref))
+        for i, ref in enumerate(blank_refs)
         for s in range(4)
     ]
 
     @pl.when(t == 0)
     def _():
-        for k in range(TILES):
+        for k in range(count):
             for move in margin_moves(k):
                 move.start()
-        zero[...] = jnp.zeros((PAD, BLOCK), bf16)
+        if blank_refs:
+            zero[...] = jnp.zeros((PAD, BLOCK), bf16)
         for move in blank_moves:
             move.start()
 
@@ -168,43 +183,41 @@
         weight = (0.1 * err_scale) + (0.25 * err_scale) * (counted * lax.rsqrt(capped))
         weight_ref[0, cut, :] = jnp.where(counted > 0.0, weight, 0.0)
 
-    @pl.when(t == TILES - 1)
-    def _():
-        for move in blank_moves:
-            move.wait()
-
-
-def ready(tile_rows, tile_cols, counts, margins):
+    if blank_refs:
+
+        @pl.when(t == count - 1)
+        def _():
+            for move in blank_moves:
+                move.wait()
+
+
+def ready(base, count, blanks, tile_rows, tile_cols, counts, margins):
     square = pl.BlockSpec((1, BLOCK, BLOCK), lambda t, *_: (t, 0, 0))
     grid_spec = pltpu.PrefetchScalarGridSpec(
         num_scalar_prefetch=2,
-        grid=(TILES,),
-        in_specs=[square, HBM],
-        out_specs=[square, square, HBM, HBM],
-        scratch_shapes=[
-            pltpu.VMEM((TILES, 2, GROUPS, LANES), f32),
+        grid=(count,),
+        in_specs=[pl.BlockSpec((1, BLOCK, BLOCK), lambda t, *_: (base + t, 0, 0)), HBM],
+        out_specs=[square, square] + [HBM] * blanks,
+        scratch_shapes=[
+            pltpu.VMEM((count, 2, GROUPS, LANES), f32),
             pltpu.VMEM((PAD, BLOCK), bf16),
             pltpu.SemaphoreType.DMA((2 * TILES + 8,)),
         ],
     )
     return pl.pallas_call(
-        ready_kernel,
+        functools.partial(ready_kernel, base, count),
         grid_spec=grid_spec,
-        out_shape=(
-            jax.ShapeDtypeStruct((TILES, BLOCK, BLOCK), f32),
-            jax.ShapeDtypeStruct((TILES, BLOCK, BLOCK), f32),
-            pltpu.HBM((4, PAD, BLOCK), bf16),
-            pltpu.HBM((4, PAD, BLOCK), bf16),
-        ),
+        out_shape=[pltpu.HBM((count, BLOCK, BLOCK), f32)] * 2
+        + [pltpu.HBM((4, PAD, BLOCK), bf16)] * blanks,
         compiler_params=pltpu.CompilerParams(
             dimension_semantics=("arbitrary",), vmem_limit_bytes=48 << 20
         ),
-        name="ready",
     )(tile_rows, tile_cols, counts, margins)
 
 
 def tile_kernel(
-    place, rows, part_ref, same_ref, other_ref, weight_ref, offset_ref, blank_ref, other_blank_ref,
+    place, rows, part_ref, same_ref, other_ref, first_weight_ref, first_offset_ref,
+    weight_ref, offset_ref, blank_ref, other_blank_ref,
     col_out_ref, keep_ref, give_ref,
     part, near, weights, offsets, col_block, row_terms, whole, col_out, sems, out_sems,
 ):
@@ -221,9 +234,12 @@
 
     def moves(k, c, width):
         cut = pl.ds(c * width, width)
+        refs, at = (first_weight_ref, first_offset_ref), k
+        if k > 0:
+            refs, at = (weight_ref, offset_ref), k - 1
         return [
-            pltpu.make_async_copy(weight_ref.at[k, cut, :], weights.at[k, cut, :], sems.at[k, 2 + c]),
-            pltpu.make_async_copy(offset_ref.at[k, cut, :], offsets.at[k, cut, :], sems.at[k, 4 + c]),
+            pltpu.make_async_copy(refs[0].at[at, cut, :], weights.at[k, cut, :], sems.at[k, 2 + c]),
+            pltpu.make_async_copy(refs[1].at[at, cut, :], offsets.at[k, cut, :], sems.at[k, 4 + c]),
         ]
 
     def out_move(k):
@@ -287,11 +303,11 @@
         out_move(k).wait()
 
 
-def tile_terms(place, tile_rows, parts, same, other, weight, offset, blank, other_blank):
+def tile_terms(place, tile_rows, parts, same, other, begun, rest):
     quad = pltpu.HBM((4, PAD, BLOCK), bf16)
     return pl.pallas_call(
         tile_kernel,
-        in_specs=[SMEM, SMEM] + [HBM] * 7,
+        in_specs=[SMEM, SMEM] + [HBM] * 9,
         out_specs=[HBM] * 3,
         scratch_shapes=[
             pltpu.VMEM((TILES, PARTS, HALF, LANES), bf16),
@@ -306,45 +322,74 @@
             pltpu.SemaphoreType.DMA((2 * TILES,)),
         ],
         out_shape=(pltpu.HBM((PARTS, TILES, HALF, LANES), bf16), quad, quad),
-        input_output_aliases={7: 1, 8: 2},
+        input_output_aliases={9: 1, 10: 2},
         compiler_params=pltpu.CompilerParams(vmem_limit_bytes=60 << 20),
         name="tile_terms",
-    )(place, tile_rows, in_hbm(parts), in_hbm(same), in_hbm(other), weight, offset, blank, other_blank)
-
-
-def join_kernel(keep_ref, got_ref, *out_refs):
-    for k in range(4):
-        out_refs[k][...] = (keep_ref[k].astype(f32) + got_ref[k].astype(f32)).astype(bf16)
+    )(place, tile_rows, in_hbm(parts), in_hbm(same), in_hbm(other), *begun, *rest)
+
+
+def settle_kernel(array_ref, out_ref):
+    del array_ref, out_ref
+
+
+def settle(array):
+    return pl.pallas_call(
+        settle_kernel,
+        out_shape=pltpu.HBM(array.shape, array.dtype),
+        in_specs=[HBM],
+        out_specs=HBM,
+        input_output_aliases={0: 0},
+        name="settle",
+    )(in_hbm(array))
+
+
+def join_kernel(keep_ref, got_ref, *refs):
+    out_refs, (keep, got, sums, sems) = refs[:4], refs[4:]
+    order = (1, 2, 3, 0)
+    moves = [
+        [
+            pltpu.make_async_copy(keep_ref.at[k], keep.at[k], sems.at[0, k]),
+            pltpu.make_async_copy(got_ref.at[k], got.at[k], sems.at[1, k]),
+        ]
+        for k in range(4)
+    ]
+    outs = [pltpu.make_async_copy(sums.at[k], out_refs[k], sems.at[2, k]) for k in range(4)]
+    for k in order:
+        for move in moves[k]:
+            move.start()
+    for k in order:
+        for move in moves[k]:
+            move.wait()
+        sums[k] = (keep[k].astype(f32) + got[k].astype(f32)).astype(bf16)
+        outs[k].start()
+    for out in outs:
+        out.wait()
 
 
 def join(keep, got):
+    quad = pltpu.VMEM((4, PAD, BLOCK), bf16)
     return pl.pallas_call(
         join_kernel,
-        out_shape=[jax.ShapeDtypeStruct((PAD, BLOCK), bf16)] * 4,
-        in_specs=[VMEM] * 2,
+        out_shape=[pltpu.HBM((PAD, BLOCK), bf16)] * 4,
+        in_specs=[HBM] * 2,
+        out_specs=[HBM] * 4,
+        scratch_shapes=[quad, quad, quad, pltpu.SemaphoreType.DMA((3, 4))],
         compiler_params=pltpu.CompilerParams(vmem_limit_bytes=16 << 20),
         name="join",
-    )(keep, got)
-
-
-def owner_sum_kernel(asked, term_ref, out_ref, terms, total, sums, sems):
+    )(in_hbm(keep), got)
+
+
+def owner_sum_kernel(asked, term_ref, out_ref, total, sums, sems):
     quarter = PARTS // 4
-    moves = []
-    for q in range(4):
-        some = pl.ds(q * quarter, quarter)
-        moves.append(pltpu.make_async_copy(term_ref.at[some], terms.at[some], sems.at[q]))
-        moves[q].start()
     total[...] = jnp.zeros((PARTS, HALF, LANES), f32)
-    for q in range(4):
-        moves[q].wait()
-        for d in range(q * quarter, (q + 1) * quarter):
-            for t in range(TILES):
-                total[asked[d, t]] += terms[d, t].astype(f32)
+    for d in range(PARTS):
+        for t in range(TILES):
+            total[asked[d, t]] += term_ref[d, t].astype(f32)
     outs = []
     for q in range(4):
         some = pl.ds(q * quarter, quarter)
         sums[some] = total[some].astype(bf16)
-        outs.append(pltpu.make_async_copy(sums.at[some], out_ref.at[some], sems.at[4 + q]))
+        outs.append(pltpu.make_async_copy(sums.at[some], out_ref.at[some], sems.at[q]))
         outs[q].start()
     for out in outs:
         out.wait()
@@ -354,17 +399,16 @@
     return pl.pallas_call(
         owner_sum_kernel,
         out_shape=pltpu.HBM((PARTS, HALF, LANES), bf16),
-        in_specs=[SMEM, HBM],
+        in_specs=[SMEM, VMEM],
         out_specs=HBM,
         scratch_shapes=[
-            pltpu.VMEM((PARTS, TILES, HALF, LANES), bf16),
             pltpu.VMEM((PARTS, HALF, LANES), f32),
             pltpu.VMEM((PARTS, HALF, LANES), bf16),
-            pltpu.SemaphoreType.DMA((8,)),
+            pltpu.SemaphoreType.DMA((4,)),
         ],
         compiler_params=pltpu.CompilerParams(vmem_limit_bytes=12 << 20),
         name="owner_sum",
-    )(asked, in_hbm(terms))
+    )(asked, in_vmem(terms))
 
 
 def adagrad(weights, history, gradient):
@@ -414,13 +458,47 @@
 
 
 def row_update_kernel(emb_ref, acc_ref, *refs):
-    grad_refs, (new_emb_ref, new_acc_ref) = refs[:4], refs[4:]
-    for n in range(GROUPS):
-        rows = span(0, DIM, n)
-        cut = slice(n * LANES, (n + 1) * LANES)
-        first, *others = [ref[:, cut].astype(f32)[0:DIM] for ref in grad_refs]
-        grad = (first + others[0]) + (others[1] + others[2])
-        new_emb_ref[rows, :], new_acc_ref[rows, :] = adagrad(emb_ref[rows, :], acc_ref[rows, :], grad)
+    grad_refs, (new_emb_ref, new_acc_ref), (held, grad, new, sems, out_sems) = (
+        refs[:4], refs[4:6], refs[6:],
+    )
+    firsts, edge = (0, ROW_CUT), (ROW_CUT, DIM - ROW_CUT)
+    cuts = [pl.ds(first * GROUPS, length * GROUPS) for first, length in zip(firsts, edge)]
+    grad_cuts = [pl.ds(0, ROW_CUT), pl.ds(ROW_CUT, PAD - ROW_CUT)]
+    moves = [
+        [
+            pltpu.make_async_copy(ref.at[cuts[h]], held.at[i, cuts[h]], sems.at[i, h])
+            for i, ref in enumerate((emb_ref, acc_ref))
+        ]
+        + [
+            pltpu.make_async_copy(ref.at[grad_cuts[h]], grad.at[i, grad_cuts[h]], sems.at[2 + i, h])
+            for i, ref in enumerate(grad_refs)
+        ]
+        for h in range(2)
+    ]
+    outs = [
+        [
+            pltpu.make_async_copy(new.at[i, cuts[h]], ref.at[cuts[h]], out_sems.at[i, h])
+            for i, ref in enumerate((new_emb_ref, new_acc_ref))
+        ]
+        for h in range(2)
+    ]
+    for h in range(2):
+        for move in moves[h]:
+            move.start()
+    for h in range(2):
+        for move in moves[h]:
+            move.wait()
+        for n in range(GROUPS):
+            rows = span(firsts[h], edge[h], n)
+            cut = slice(n * LANES, (n + 1) * LANES)
+            parts = [grad[i, grad_cuts[h], cut].astype(f32)[0 : edge[h]] for i in range(4)]
+            total = (parts[0] + parts[1]) + (parts[2] + parts[3])
+            new[0, rows, :], new[1, rows, :] = adagrad(held[0, rows, :], held[1, rows, :], total)
+        for out in outs[h]:
+            out.start()
+    for h in range(2):
+        for out in outs[h]:
+            out.wait()
 
 
 def row_update(emb, acc, grads):
@@ -428,10 +506,18 @@
     new_emb, new_acc = pl.pallas_call(
         row_update_kernel,
         out_shape=(shape, shape),
-        in_specs=[VMEM] * 6,
+        in_specs=[HBM] * 6,
+        out_specs=[HBM, HBM],
+        scratch_shapes=[
+            pltpu.VMEM((2, GROUPS * DIM, LANES), f32),
+            pltpu.VMEM((4, PAD, BLOCK), bf16),
+            pltpu.VMEM((2, GROUPS * DIM, LANES), f32),
+            pltpu.SemaphoreType.DMA((6, 2)),
+            pltpu.SemaphoreType.DMA((2, 2)),
+        ],
         compiler_params=pltpu.CompilerParams(vmem_limit_bytes=16 << 20),
         name="row_update",
-    )(emb, acc, *grads)
+    )(in_hbm(emb), in_hbm(acc), in_hbm(grads[0]), *grads[1:])
     return new_emb.reshape(1, DIM, BLOCK), new_acc.reshape(1, DIM, BLOCK)
 
 
@@ -453,14 +539,14 @@
     row_low = lower(row_emb)
     held = lax.all_to_all(slices, "row", 0, 0, tiled=True)
     near = [row_low] + [send_along_z(row_low, step) for step in (1, 2, 3)]
-    weight, offset, blank, other_blank = ready(tile_rows, tile_cols, counts, margins)
+    begun = ready(0, 1, 0, tile_rows, tile_cols, counts, margins)
+    rest = ready(1, TILES - 1, 2, tile_rows, tile_cols, counts, margins)
     picked, asked = pick(held)
     parts = lax.all_to_all(picked, "row", 0, 0, tiled=True)
     same = jnp.concatenate(near, axis=0)
     other = swap_cores(same)
-    terms, keep, give = tile_terms(
-        place, tile_rows, parts, same, other, weight, offset, blank, other_blank
-    )
+    other = settle(other)
+    terms, keep, give = tile_terms(place, tile_rows, parts, same, other, begun, rest)
     got = swap_cores(give)
     terms = lax.all_to_all(terms, "row", 0, 0, tiled=True)
     grads = join(keep, got)

time: 171 us -> 171 us (level)
  Pallas kernels: 46.4 us -> 51.3 us
  waiting for transfers between devices: 66.6 us -> 62.8 us
    pallas_call x5 -> x7, Pallas kernels: 37.8 us -> 43.9 us  [the longest x2 18.2 us: ready(): pl.pallas_call(functools.partial(ready_kernel, base, count), grid_spec=gr...]
    all_to_all x1, waiting for transfers between devices: 12.8 us -> 9.61 us  [body(): parts = lax.all_to_all(picked, 'row', 0, 0, tiled=True)]
  transfers between devices with their start and end apart: 10 -> 10, of which waited for: 5 -> 5; matrix products, arithmetic and copies ran while one was open for 0% -> 0% of each run, Pallas kernels for 17% -> 19%
where the time goes in v4:
time: 171 us
  waiting for transfers between devices  62.8 us (37%)
  Pallas kernels  51.3 us (30%)
  blocking collectives  36.8 us (22%)
  starting transfers between devices  17.1 us (10%)
    ppermute x6, waiting for transfers between devices, send_along_z(): lax.ppermute(array, 'col', [(i, (i + 2 * step) % COLS) for i in range(COL...  28.8 us
    all_to_all x1, waiting for transfers between devices, body(): terms = lax.all_to_all(terms, 'row', 0, 0, tiled=True)  23.1 us
    all_to_all x1, blocking collectives, body(): held = lax.all_to_all(slices, 'row', 0, 0, tiled=True)  20.6 us
    pallas_call x2, Pallas kernels, ready(): pl.pallas_call(functools.partial(ready_kernel, base, count), grid_spec=gr...  18.2 us
    all_to_all x1, blocking collectives, body(): col_sum = lax.all_to_all(sums, 'row', 0, 0, tiled=True)  16.2 us
    pallas_call x1, Pallas kernels, tile_terms(): pl.pallas_call(tile_kernel, in_specs=[SMEM, SMEM] + [HBM] * 9, out_specs=...  15.3 us
    all_to_all x1, waiting for transfers between devices, body(): parts = lax.all_to_all(picked, 'row', 0, 0, tiled=True)  9.61 us
    ppermute x6, starting transfers between devices, send_along_z(): lax.ppermute(array, 'col', [(i, (i + 2 * step) % COLS) for i in range(COL...  8.78 us
  transfers between devices with their start and end apart: 10, of which 5 were waited for; matrix products, arithmetic and copies ran while one was open for 0% of the time, Pallas kernels for 19%

profile of v4, /device:TPU:0, one launch (start us, length us, event | category | flops | bytes accessed | tf_op | source)
XLA Modules:
  0.0 170.6 jit_solution(6904367432069505814)
XLA Ops:
  0.6 0.0 copy-start
  0.6 1.3 copy-done
  1.9 0.3 lower.1
  2.2 4.2 %collective-permute-start.2 = (bf16[1,304,1024]{2,1,0:T(8,128)(2,1)S(1)}, bf16[1,304,1024]{2,1,0:T(8,128)(2,1)S(1)}, u32[]{:S(2)}, u32[]{:S(2)}) collective-permute-start(bf16[1,304,1024]{2,1,0:T(8,128)(2,1)S(1)} %lower.1), channel_id=1, source_target_pairs={{0,6},{1,7},{2,0},{3,1},{4,2},{5,3},{6,4},{7,5},{8,14},{9,15},{10,... | collective-permute-start | bytes 1867784 | tf_op jit(solution)/shard_map/ppermute | solution.py:525
  6.4 0.0 collective-permute-start.1
  6.4 1.3 collective-permute-start
  7.7 25.4 %collective-permute-done.2 = bf16[1,304,1024]{2,1,0:T(8,128)(2,1)S(1)} collective-permute-done((bf16[1,304,1024]{2,1,0:T(8,128)(2,1)S(1)}, bf16[1,304,1024]{2,1,0:T(8,128)(2,1)S(1)}, u32[]{:S(2)}, u32[]{:S(2)}) %collective-permute-start.2) | collective-permute-done | bytes 622624 | tf_op jit(solution)/shard_map/ppermute | solution.py:525
  33.0 3.4 %collective-permute-done = bf16[1,304,1024]{2,1,0:T(8,128)(2,1)S(1)} collective-permute-done((bf16[1,304,1024]{2,1,0:T(8,128)(2,1)S(1)}, bf16[1,304,1024]{2,1,0:T(8,128)(2,1)S(1)}, u32[]{:S(2)}, u32[]{:S(2)}) %collective-permute-start) | collective-permute-done | bytes 622624 | tf_op jit(solution)/shard_map/ppermute | solution.py:525
  36.5 0.3 pad_maximum_fusion.same_ref
  36.8 0.1 collective-permute-start.3
  36.9 2.9 %cut_up.1 = bf16[8,2,160,128]{3,2,1,0:T(8,128)(2,1)} custom-call(s32[3]{0:T(128)} %cols.3, f32[2400,128]{1,0:T(8,128)} %bitcast.15), custom_call_target="tpu_custom_call" | custom-call | tf_op jit(solution)/shard_map/cut_up/pallas_call | solution.py:77
  39.7 20.6 %all_to_all.20.held_ref = bf16[16,160,128]{2,1,0:T(8,128)(2,1)S(1)} all-to-all(bf16[16,160,128]{2,1,0:T(8,128)(2,1)} %bitcast.17), channel_id=1, replica_groups=mesh['row'=16,'col'=8] {'row'}, dimensions={0} | all-to-all | bytes 1310720 | tf_op jit(solution)/shard_map/all_to_all | solution.py:540
  60.3 2.0 %pick.1 = (bf16[16,3,152,128]{3,2,1,0:T(8,128)(2,1)}, s32[16,128]{1,0:T(8,128)S(1)}) custom-call(bf16[16,160,128]{2,1,0:T(8,128)(2,1)S(1)} %all_to_all.20.held_ref), custom_call_target="tpu_custom_call" | custom-call | tf_op jit(solution)/shard_map/pick/pallas_call | solution.py:129
  62.3 4.4 %all-to-all-start.1 = ((bf16[16,3,152,128]{3,2,1,0:T(8,128)(2,1)}), bf16[16,3,152,128]{3,2,1,0:T(8,128)(2,1)}, u32[]{:S(2)}, u32[]{:S(2)}) async-start(bf16[16,3,152,128]{3,2,1,0:T(8,128)(2,1)} %get-tuple-element.23), calls=%async_computation.1 | async-start | bytes 3735552 | tf_op jit(solution)/shard_map/all_to_all | solution.py:545
  66.8 7.8 %shard_map.111 = (f32[1,1024,1024]{2,1,0:T(8,128)}, f32[1,1024,1024]{2,1,0:T(8,128)}) custom-call(s32[3]{0:T(128)S(1)} %copy-done.2, s32[3]{0:T(128)S(1)} %copy-done.3, s32[3,1024,1024]{2,1,0:T(8,128)} %count_ref.3, f32[128,8,128]{2,1,0:T(8,128)S(1)} %bitcast.13), custom_call_target="tpu_custom_call" | custom-call | tf_op jit(solution)/shard_map/pallas_call | solution.py:207
  74.6 10.3 %shard_map.112 = (f32[2,1024,1024]{2,1,0:T(8,128)}, f32[2,1024,1024]{2,1,0:T(8,128)}, bf16[4,304,1024]{2,1,0:T(8,128)(2,1)}, bf16[4,304,1024]{2,1,0:T(8,128)(2,1)}) custom-call(s32[3]{0:T(128)S(1)} %copy-done.2, s32[3]{0:T(128)S(1)} %copy-done.3, s32[3,1024,1024]{2,1,0:T(8,128)} %count_ref.3, f32[128,8,128]{2,1,0:T(8,128)S(1)} %bitcast.14), custom_call_target="tpu_custom_call" | custom-call | tf_op jit(solution)/shard_map/pallas_call | solution.py:207
  85.0 0.0 collective-permute-done.3.array_ref
  85.0 9.6 %all-to-all-done.1.part_ref = bf16[16,3,152,128]{3,2,1,0:T(8,128)(2,1)} async-done(((bf16[16,3,152,128]{3,2,1,0:T(8,128)(2,1)}), bf16[16,3,152,128]{3,2,1,0:T(8,128)(2,1)}, u32[]{:S(2)}, u32[]{:S(2)}) %all-to-all-start.1) | async-done | bytes 1867808 | tf_op jit(solution)/shard_map/all_to_all | solution.py:545
  94.6 15.3 %tile_terms.1 = (bf16[16,3,152,128]{3,2,1,0:T(8,128)(2,1)}, bf16[4,304,1024]{2,1,0:T(8,128)(2,1)}, bf16[4,304,1024]{2,1,0:T(8,128)(2,1)}) custom-call(s32[1]{0:T(128)} %bitcast.2.place, s32[3]{0:T(128)} %rows.5, bf16[16,3,152,128]{3,2,1,0:T(8,128)(2,1)} %all-to-all-done.1.part_ref, ...), custom_call_target="tpu_custom_call", output_to_operand_aliasing={{1}: (9, {}), {2}: (10, {})} | custom-call | tf_op jit(solution)/shard_map/tile_terms/pallas_call | solution.py:308
  110.0 0.1 collective-permute-start.4
  110.1 3.7 %all-to-all-start.2 = ((bf16[16,3,152,128]{3,2,1,0:T(8,128)(2,1)}), bf16[16,3,152,128]{3,2,1,0:T(8,128)(2,1)S(1)}, u32[]{:S(2)}, u32[]{:S(2)}) async-start(bf16[16,3,152,128]{3,2,1,0:T(8,128)(2,1)} %get-tuple-element.38), calls=%async_computation.2 | async-start | bytes 3735552 | tf_op jit(solution)/shard_map/all_to_all | solution.py:551
  113.8 1.3 collective-permute-done.4.got_ref
  115.1 3.7 %join.1 = (bf16[304,1024]{1,0:T(8,128)(2,1)}, bf16[304,1024]{1,0:T(8,128)(2,1)}, bf16[304,1024]{1,0:T(8,128)(2,1)}, bf16[304,1024]{1,0:T(8,128)(2,1)}) custom-call(bf16[4,304,1024]{2,1,0:T(8,128)(2,1)} %get-tuple-element.30.keep_ref, bf16[4,304,1024]{2,1,0:T(8,128)(2,1)} %collective-permute-done.4.got_ref), custom_call_target="tpu_custom_call" | custom-call | tf_op jit(solution)/shard_map/join/pallas_call | solution.py:371
  118.8 0.1 collective-permute-start.5
  118.9 2.3 %collective-permute-start.6 = (bf16[304,1024]{1,0:T(8,128)(2,1)}, bf16[304,1024]{1,0:T(8,128)(2,1)S(1)}, u32[]{:S(2)}, u32[]{:S(2)}) collective-permute-start(bf16[304,1024]{1,0:T(8,128)(2,1)} %get-tuple-element.34), channel_id=1, source_target_pairs={{0,4},{1,5},{2,6},{3,7},{4,0},{5,1},{6,2},{7,3},{8,12},{9,13},{10,... | collective-permute-start | bytes 1867784 | tf_op jit(solution)/shard_map/ppermute | solution.py:525
  121.2 0.9 collective-permute-start.7
  122.1 23.1 %all-to-all-done.2.term_ref = bf16[16,3,152,128]{3,2,1,0:T(8,128)(2,1)S(1)} async-done(((bf16[16,3,152,128]{3,2,1,0:T(8,128)(2,1)}), bf16[16,3,152,128]{3,2,1,0:T(8,128)(2,1)S(1)}, u32[]{:S(2)}, u32[]{:S(2)}) %all-to-all-start.2) | async-done | bytes 1867808 | tf_op jit(solution)/shard_map/all_to_all | solution.py:551
  145.2 2.0 %owner_sum.1 = bf16[16,152,128]{2,1,0:T(8,128)(2,1)} custom-call(s32[16,128]{1,0:T(8,128)S(1)} %get-tuple-element.37.asked, bf16[16,3,152,128]{3,2,1,0:T(8,128)(2,1)S(1)} %all-to-all-done.2.term_ref), custom_call_target="tpu_custom_call" | custom-call | tf_op jit(solution)/shard_map/owner_sum/pallas_call | solution.py:399
  147.2 16.2 %all_to_all.21.grad_ref = bf16[16,152,128]{2,1,0:T(8,128)(2,1)S(1)} all-to-all(bf16[16,152,128]{2,1,0:T(8,128)(2,1)} %owner_sum.1), channel_id=1, replica_groups=mesh['row'=16,'col'=8] {'row'}, dimensions={0} | all-to-all | bytes 1245184 | tf_op jit(solution)/shard_map/all_to_all | solution.py:555
  163.4 3.2 %col_update.1 = (f32[2400,128]{1,0:T(8,128)}, f32[2400,128]{1,0:T(8,128)}) custom-call(f32[2400,128]{1,0:T(8,128)} %bitcast.16, f32[2400,128]{1,0:T(8,128)} %bitcast.18, bf16[16,152,128]{2,1,0:T(8,128)(2,1)S(1)} %all_to_all.21.grad_ref), custom_call_target="tpu_custom_call" | custom-call | tf_op jit(solution)/shard_map/col_update/pallas_call | solution.py:443
  166.6 0.0 collective-permute-done.5.refs_1_
  166.7 3.8 %row_update.1 = (f32[2400,128]{1,0:T(8,128)}, f32[2400,128]{1,0:T(8,128)}) custom-call(f32[2400,128]{1,0:T(8,128)} %bitcast.11, f32[2400,128]{1,0:T(8,128)} %bitcast.19, bf16[304,1024]{1,0:T(8,128)(2,1)} %get-tuple-element.32.refs_0_, bf16[304,1024]{1,0:T(8,128)(2,1)S(1)} %collective-permute-done.5.refs_1_, ...), custom_call_target="tpu_custom_call" | custom-call | tf_op jit(solution)/shard_map/row_update/pallas_call | solution.py:506
  (12 shorter events, 0.0 us)
Async XLA Ops:
  0.6 1.3 copy-start
  2.2 30.8 %collective-permute-start.2 = (bf16[1,304,1024]{2,1,0:T(8,128)(2,1)S(1)}, bf16[1,304,1024]{2,1,0:T(8,128)(2,1)S(1)}, u32[]{:S(2)}, u32[]{:S(2)}) collective-permute-start(bf16[1,304,1024]{2,1,0:T(8,128)(2,1)S(1)} %lower.1), channel_id=1, source_target_pairs={{0,6},{1,7},{2,0},{3,1},{4,2},{5,3},{6,4},{7,5},{8,14},{9,15},{10,... | collective-permute-start | bytes 1867784 | tf_op jit(solution)/shard_map/ppermute | solution.py:525
  6.4 26.6 %collective-permute-start.1 = (bf16[1,304,1024]{2,1,0:T(8,128)(2,1)S(1)}, bf16[1,304,1024]{2,1,0:T(8,128)(2,1)S(1)}, u32[]{:S(2)}, u32[]{:S(2)}) collective-permute-start(bf16[1,304,1024]{2,1,0:T(8,128)(2,1)S(1)} %lower.1), channel_id=1, source_target_pairs={{0,4},{1,5},{2,6},{3,7},{4,0},{5,1},{6,2},{7,3},{8,12},{9,13},{10,... | collective-permute-start | bytes 1867784 | tf_op jit(solution)/shard_map/ppermute | solution.py:525
  6.4 30.0 %collective-permute-start = (bf16[1,304,1024]{2,1,0:T(8,128)(2,1)S(1)}, bf16[1,304,1024]{2,1,0:T(8,128)(2,1)S(1)}, u32[]{:S(2)}, u32[]{:S(2)}) collective-permute-start(bf16[1,304,1024]{2,1,0:T(8,128)(2,1)S(1)} %lower.1), channel_id=1, source_target_pairs={{0,2},{1,3},{2,4},{3,5},{4,6},{5,7},{6,0},{7,1},{8,10},{9,11},{10,... | collective-permute-start | bytes 1867784 | tf_op jit(solution)/shard_map/ppermute | solution.py:525
  36.8 25.5 %copy-start.4 = (bf16[4,304,1024]{2,1,0:T(8,128)(2,1)}, bf16[4,304,1024]{2,1,0:T(8,128)(2,1)S(1)}, u32[]{:S(2)}) copy-start(bf16[4,304,1024]{2,1,0:T(8,128)(2,1)S(1)} %pad_maximum_fusion.same_ref) | copy-start | bytes 7471108
  36.8 48.2 %collective-permute-start.3 = (bf16[4,304,1024]{2,1,0:T(8,128)(2,1)S(1)}, bf16[4,304,1024]{2,1,0:T(8,128)(2,1)}, u32[]{:S(2)}, u32[]{:S(2)}) collective-permute-start(bf16[4,304,1024]{2,1,0:T(8,128)(2,1)S(1)} %pad_maximum_fusion.same_ref), channel_id=1, source_target_pairs={{0,1},{1,0},{2,3},{3,2},{4,5},{5,4},{6,7},{7,6},{8,9},{9,8},{10,11... | collective-permute-start | bytes 7471112 | tf_op jit(solution)/shard_map/ppermute | solution.py:529
  60.3 6.5 %copy-start.1 = (f32[131072]{0:T(1024)S(1)}, f32[131072]{0:T(1024)}, u32[]{:S(2)}) copy-start(f32[131072]{0:T(1024)} %param.12) | copy-start | bytes 1572868
  60.3 6.5 %copy-start.2 = (s32[3]{0:T(128)S(1)}, s32[3]{0:T(128)}, u32[]{:S(2)}) copy-start(s32[3]{0:T(128)} %rows.5) | copy-start | bytes 40
  60.3 6.5 %copy-start.3 = (s32[3]{0:T(128)S(1)}, s32[3]{0:T(128)}, u32[]{:S(2)}) copy-start(s32[3]{0:T(128)} %cols.3) | copy-start | bytes 40
  62.3 32.3 %all-to-all-start.1 = ((bf16[16,3,152,128]{3,2,1,0:T(8,128)(2,1)}), bf16[16,3,152,128]{3,2,1,0:T(8,128)(2,1)}, u32[]{:S(2)}, u32[]{:S(2)}) async-start(bf16[16,3,152,128]{3,2,1,0:T(8,128)(2,1)} %get-tuple-element.23), calls=%async_computation.1 | async-start | bytes 3735552 | tf_op jit(solution)/shard_map/all_to_all | solution.py:545
  110.0 5.1 %collective-permute-start.4 = (bf16[4,304,1024]{2,1,0:T(8,128)(2,1)}, bf16[4,304,1024]{2,1,0:T(8,128)(2,1)}, u32[]{:S(2)}, u32[]{:S(2)}) collective-permute-start(bf16[4,304,1024]{2,1,0:T(8,128)(2,1)} %get-tuple-element.31), channel_id=1, source_target_pairs={{0,1},{1,0},{2,3},{3,2},{4,5},{5,4},{6,7},{7,6},{8,9},{9,8},{10,11... | collective-permute-start | bytes 7471112 | tf_op jit(solution)/shard_map/ppermute | solution.py:529
  110.1 35.2 %all-to-all-start.2 = ((bf16[16,3,152,128]{3,2,1,0:T(8,128)(2,1)}), bf16[16,3,152,128]{3,2,1,0:T(8,128)(2,1)S(1)}, u32[]{:S(2)}, u32[]{:S(2)}) async-start(bf16[16,3,152,128]{3,2,1,0:T(8,128)(2,1)} %get-tuple-element.38), calls=%async_computation.2 | async-start | bytes 3735552 | tf_op jit(solution)/shard_map/all_to_all | solution.py:551
  118.8 47.8 %collective-permute-start.5 = (bf16[304,1024]{1,0:T(8,128)(2,1)}, bf16[304,1024]{1,0:T(8,128)(2,1)S(1)}, u32[]{:S(2)}, u32[]{:S(2)}) collective-permute-start(bf16[304,1024]{1,0:T(8,128)(2,1)} %get-tuple-element.33), channel_id=1, source_target_pairs={{0,2},{1,3},{2,4},{3,5},{4,6},{5,7},{6,0},{7,1},{8,10},{9,11},{10,... | collective-permute-start | bytes 1867784 | tf_op jit(solution)/shard_map/ppermute | solution.py:525
  118.9 47.8 %collective-permute-start.6 = (bf16[304,1024]{1,0:T(8,128)(2,1)}, bf16[304,1024]{1,0:T(8,128)(2,1)S(1)}, u32[]{:S(2)}, u32[]{:S(2)}) collective-permute-start(bf16[304,1024]{1,0:T(8,128)(2,1)} %get-tuple-element.34), channel_id=1, source_target_pairs={{0,4},{1,5},{2,6},{3,7},{4,0},{5,1},{6,2},{7,3},{8,12},{9,13},{10,... | collective-permute-start | bytes 1867784 | tf_op jit(solution)/shard_map/ppermute | solution.py:525
  121.2 45.5 %collective-permute-start.7 = (bf16[304,1024]{1,0:T(8,128)(2,1)}, bf16[304,1024]{1,0:T(8,128)(2,1)}, u32[]{:S(2)}, u32[]{:S(2)}) collective-permute-start(bf16[304,1024]{1,0:T(8,128)(2,1)} %get-tuple-element.35), channel_id=1, source_target_pairs={{0,6},{1,7},{2,0},{3,1},{4,2},{5,3},{6,4},{7,5},{8,14},{9,15},{10,... | collective-permute-start | bytes 1867784 | tf_op jit(solution)/shard_map/ppermute | solution.py:525
